TPU v7x, 32 devices: a whole 2x2x4 slice. The times are simulated.
32 devices in a mesh: grp: 2 (over y), strm: 8 (over z, x), azim: 2 (over core).
Axes of the slice: x: 2, y: 2, z: 4, core: 2. Of those that a mesh axis runs over, the one named last changes fastest.
Arguments:
- fields: bfloat16 [7, 512, 4096], P(None, None, ('grp', 'strm', 'azim')), parts along dimension 2, may hold values from -6 to 6
- elem_map: int32 [16, 128], P(('strm', 'azim')), may hold values from 0 to 127, each once within a row
- metric: float32 [3, 2048], P(None, ('strm', 'azim')), may hold values from 0.5 to 2
- inv_reynolds: float32 [2], P('grp'), parts along dimension 0, may hold values from 0.005 to 0.05
Outputs:
- indicator: float32 [4096], P(('grp', 'strm', 'azim')), parts along dimension 0
There are 2 independent parts, one for each index of `grp`. A program takes and returns all parts, laid end to end along the dimension named above; an argument that names none is the same for every part. Nothing has to cross between parts.
Inputs may be any that keep to these rules, and one draw needn't show every extreme that they name: Each row of elem_map holds each of 0 to 127 once.
All inputs are finite; a program needn't handle non-finite values.
Results may differ from a plain program's by a relative error of at most 0.0003.
Values may be sent and summed in bfloat16 or wider, within the bound.
No kernel may reach another device: no remote copies, remote signals or barrier semaphores. Data moves between devices by JAX's collectives and lax.ppermute only.
A program may use at most 128 MiB of HBM per device.

v0:
```python
import functools

import jax
import jax.numpy as jnp
import numpy as np
from jax import lax
from jax.experimental import pallas as pl
from jax.experimental.pallas import tpu as pltpu
from jax.sharding import PartitionSpec as P

ORDER_IN = 7
ORDER_OUT = 9
EY = 8
EZ = 8
NI = ORDER_IN + 1
NO = ORDER_OUT + 1
HI = NI // 2
HO = NO // 2
ROWS = 128
EXT = NI + 2
SEAM = EXT * NI
BF = jnp.bfloat16
F32 = jnp.float32
PLACE = {3: (0, 0), 4: (0, 1), 5: (1, 0), 6: (1, 1), 0: (2, 0), 1: (2, 1), 2: (3, 0)}


def gll_table(extent):
    degree = extent - 1
    points = np.cos(np.pi * np.arange(extent) / degree)
    legendre = np.zeros((extent, extent))

    def fill():
        legendre[:, 0] = 1.0
        legendre[:, 1] = points
        for level in range(2, extent):
            legendre[:, level] = (
                (2 * level - 1) * points * legendre[:, level - 1]
                - (level - 1) * legendre[:, level - 2]
            ) / level

    for sweep in range(100):
        fill()
        points = points - (points * legendre[:, degree] - legendre[:, degree - 1]) / (
            extent * legendre[:, degree]
        )
    fill()
    weights = 2.0 / (degree * extent * legendre[:, degree] ** 2)
    return (points[::-1].copy(), weights[::-1].copy())


def lagrange_matrix(source, target):
    result = np.ones((len(target), len(source)))
    for column in range(len(source)):
        for partner in range(len(source)):
            if partner != column:
                result[:, column] *= (target - source[partner]) / (source[column] - source[partner])
    return result


def derivative_matrix(points):
    extent = len(points)
    identity = np.eye(extent)
    spacing = points[:, None] - points[None, :] + identity
    barycen = 1.0 / np.prod(spacing, axis=1)
    matrix = barycen[None, :] / barycen[:, None] / spacing * (1.0 - identity)
    return matrix - identity * matrix.sum(axis=1)[:, None]


def bf16_parts(matrix):
    high = matrix.astype(jnp.bfloat16)
    low = (matrix - high.astype(np.float64)).astype(jnp.bfloat16)
    return high, low


def pad_rows(matrix, rows):
    return np.concatenate([matrix, np.zeros((rows - matrix.shape[0],) + matrix.shape[1:])])


def two_terms(matrix):
    return np.concatenate(bf16_parts(matrix), axis=-1)


@functools.cache
def tables():
    coarse, unused = gll_table(NI)
    fine, weights = gll_table(NO)
    interp = lagrange_matrix(coarse, fine)
    slopes = derivative_matrix(fine)
    ends = np.eye(NO)[:, [0, NO - 1]]
    value = np.concatenate([interp, ends], axis=1)
    both = slopes @ value

    def folded(matrix, parity):
        sign = 1.0 - 2.0 * parity
        if matrix.shape[1] == EXT and matrix is not slopes:
            left = matrix[:HO, [0, 1, 2, 3, 8]]
            right = matrix[:HO, [7, 6, 5, 4, 9]]
        else:
            left = matrix[:HO, :HO]
            right = matrix[:HO, ::-1][:, :HO]
        return left + sign * right

    refine = []
    for sector in range(8):
        pa, pb, pc = sector // 4, sector // 2 % 2, sector % 2
        blocks = []
        for ta, tb, tc in (
            (value, value, value),
            (both, value, value),
            (value, both, value),
            (value, value, both),
        ):
            block = 0.125 * np.einsum(
                "ap,bq,cr->abcrpq", folded(ta, pa), folded(tb, pb), folded(tc, pc)
            ).reshape(HO**3, HO, HO * HO)
            main = block[:, :, : HO * HO - 1].reshape(HO**3, -1)
            tail = np.pad(block[:, :, HO * HO - 1], ((0, 0), (0, ROWS - main.shape[1] - HO)))
            blocks.append(pad_rows(np.concatenate([main, tail], axis=1), ROWS))
        refine.append(two_terms(np.concatenate(blocks)))
    refine = np.stack(refine)

    second = []
    eye = np.eye(HO)
    for axis in range(3):
        for parity in range(2):
            factors = [eye, eye, eye]
            factors[axis] = folded(slopes, parity)
            block = np.kron(np.kron(factors[0], factors[1]), factors[2])
            edge = ROWS - HO**3
            second.append(two_terms(np.pad(block, ((0, edge), (0, edge)))))
    second = np.stack(second)

    def half(side):
        return value[:HO] if side == 0 else value[::-1][:HO]

    lift_x, lift_y = [], []
    for side in range(2):
        for radial in range(2):
            plain = np.zeros((HO, EXT, HO, NI))
            added = np.zeros((HO, EXT, HO, NI))
            plain[...] = np.einsum("ap,cr->apcr", half(side), half(radial)[:, :NI])
            added[..., 0] = np.einsum("ap,c->apc", half(side), half(radial)[:, NI])
            added[..., NI - 1] = np.einsum("ap,c->apc", half(side), half(radial)[:, NI + 1])
            face = np.stack([plain, added]).transpose(1, 3, 0, 2, 4).reshape(HO, HO, 2 * SEAM)
            lift_x.append(pad_rows(face.reshape(HO * HO, -1), 32))
            spread = np.zeros((HO, HO, HO, 2 * SEAM))
            spread[:, 0] = face
            lift_y.append(pad_rows(spread.reshape(HO**3, -1), ROWS))
    lift_x = two_terms(np.concatenate(lift_x))
    lift_y = two_terms(np.concatenate(lift_y))

    half_weights = weights[:HO]
    quad = np.kron(np.kron(half_weights, half_weights), half_weights)[:, None]
    quad = np.broadcast_to(pad_rows(quad, ROWS), (ROWS, 128)).astype(np.float32)
    line = []
    for end, far in ((0, NO - 1), (NO - 1, 0)):
        weights_in = slopes[end].copy()
        weights_in[[0, NO - 1]] = 0.0
        line.append(([float(v) for v in weights_in @ interp], float(slopes[end, far])))
    ends = (float(slopes[0, 0]), float(slopes[NO - 1, NO - 1]))
    return refine, second, lift_x, lift_y, quad, (line, ends)


def dot(a, b, contract_last=False):
    dims = (((1,), (1 if contract_last else 0,)), ((), ()))
    return lax.dot_general(a, b, dims, preferred_element_type=F32)


def rows3(x):
    return x.reshape(NI, NI, x.shape[-1])


def seam_rows(x):
    return x.reshape(SEAM, x.shape[-1])


def rows2(x):
    return x.reshape(NI * NI, x.shape[-1])


def roll(x, shift):
    count = x.shape[-1]
    return pltpu.roll(x, shift % count, x.ndim - 1)


def positions(shape):
    lane = lax.broadcasted_iota(jnp.int32, shape, len(shape) - 1)
    return lax.div(lane, EY * EZ), lax.rem(lax.div(lane, EZ), EY), lax.rem(lane, EZ)


def split3(x):
    high = x.astype(BF)
    rest = x - high.astype(F32)
    mid = rest.astype(BF)
    low = (rest - mid.astype(F32)).astype(BF)
    return high, mid, low


def slot_matrix(emap_ref, count):
    local = lax.broadcasted_iota(jnp.int32, (count, count), 0)
    return (local == emap_ref[...]).astype(F32).astype(BF)


def radial_added(x):
    axis = x.ndim - 2
    shape = (1,) * axis + x.shape[-2:]
    node = lax.broadcasted_iota(jnp.int32, shape, axis)
    iz = positions(shape)[2]
    last = x.shape[-2] - 1
    before = pltpu.roll(roll(x, 1), 1, axis)
    after = pltpu.roll(roll(x, -1), last, axis)
    low = (node == 0) & (iz > 0)
    high = (node == last) & (iz < EZ - 1)
    other = jnp.where(low, before, jnp.where(high, after, x))
    return 0.5 * (other - x)


def end_lines(line, planes, step):
    (near, near_far), (high, high_far) = line
    first, last = planes[0], planes[-1]
    one = near_far * 0.5 * (last + roll(first, -step))
    two = high_far * 0.5 * (first + roll(last, step))
    for i, plane in enumerate(planes):
        one = one + near[i] * plane
        two = two + high[i] * plane
    return one, two


def first_kernel(line, fields_ref, emap_ref, metric_ref, coarse_ref, metric_out, msg_ref):
    count = fields_ref.shape[-1]
    slots = slot_matrix(emap_ref, count)
    high, mid, low = split3(metric_ref[...])
    pad = jnp.zeros((7, count), F32)
    stacked = jnp.concatenate([high.astype(F32), mid.astype(F32), low.astype(F32), pad], axis=0)
    moved = dot(stacked.astype(BF), slots, True)
    local = moved[0:3] + moved[3:6] + moved[6:9]
    metric_out[...] = jnp.concatenate([local, jnp.zeros((5, count), F32)], axis=0)
    high = local.astype(BF).astype(F32)
    tail = jnp.concatenate([high, local - high, jnp.zeros((10, count), F32)], axis=0)
    msg_ref[9 * 64 : 9 * 64 + 16, :] = tail.astype(BF)
    iy = positions((1, 1, count))[1]
    for f in range(7):
        values = dot(fields_ref[f], slots, True).reshape(NI, NI, NI, count)
        coarse_ref[f] = values
        face = jnp.where(iy == 0, values[:, 0], values[:, NI - 1])
        msg_ref[f * 64 : f * 64 + 64, :] = rows2(face).astype(BF)
        if f in (3, 5):
            low, high = end_lines(line, [values[:, b] for b in range(NI)], EZ)
            at = (7 + (f == 5)) * 64
            msg_ref[at : at + 64, :] = rows2(jnp.where(iy == 0, low, high)).astype(BF)


def from_azim(x, iy):
    gap = (EY - 1) * EZ
    return jnp.where(iy == 0, roll(x, -gap), roll(x, gap))


def metric_classes(x, halo, shift, at_low, at_high):
    low = 0.5 * (x + jnp.where(at_low, halo, roll(x, shift)))
    high = 0.5 * (x + jnp.where(at_high, halo, roll(x, -shift)))
    return [x, low, high]


def radial_classes(x, iz):
    low = jnp.where(iz > 0, 0.5 * (x + roll(x, 1)), x)
    high = jnp.where(iz < EZ - 1, 0.5 * (x + roll(x, -1)), x)
    return [x, low, high]


def second_kernel(
    line, par_ref, coarse_ref, metric_ref, halo_ref, ext_ref, ends_ref, table_ref, a_ref, b_ref
):
    count = coarse_ref.shape[-1]
    layer = EY * EZ
    ix, iy, iz = positions((1, 1, count))
    blocks = []
    lines = []
    for f in range(7):
        values = coarse_ref[f]
        first, last = values[:, 0], values[:, NI - 1]
        halo = from_azim(rows3(halo_ref[f * 64 : f * 64 + 64, :].astype(F32)), iy)
        low = 0.5 * (jnp.where(iy == 0, halo, roll(last, EZ)) - first)
        high = 0.5 * (jnp.where(iy == EY - 1, halo, roll(first, -EZ)) - last)
        values = jnp.concatenate([values, low[:, None], high[:, None]], axis=1)
        ext_ref[f] = values
        blocks.append(seam_rows(jnp.where(ix == 0, values[0], values[NI - 1])))
        if f in (4, 5):
            low, high = end_lines(line, [values[a] for a in range(NI)], layer)
            lines.append(seam_rows(jnp.where(ix == 0, low, high)))
    blocks += lines
    extra = []
    for i in range(2):
        ends = from_azim(rows3(halo_ref[(7 + i) * 64 : (8 + i) * 64, :].astype(F32)), iy)
        ends_ref[i] = ends
        extra.append(jnp.where(ix[0] == 0, ends[0], ends[NI - 1]))

    ix, iy, iz = positions((1, count))
    packed = halo_ref[9 * 64 : 9 * 64 + 16, :].astype(F32)
    other = from_azim(packed[0:3] + packed[3:6], iy)
    own = metric_ref[...]
    lows, highs = iy == 0, iy == EY - 1
    rows = []
    for item in metric_classes(own[0:1], other[0:1], EZ, lows, highs):
        rows += radial_classes(item, iz)
    rows += radial_classes(own[1:2], iz)
    rows += metric_classes(own[2:3], other[2:3], EZ, lows, highs)
    rows += radial_classes(other[1:2], iz)
    table = jnp.concatenate(rows + [jnp.zeros((24 - len(rows), count), F32)], axis=0)
    table_ref[...] = table
    high = table.astype(BF).astype(F32)
    spare = jnp.zeros((SEAM - 64, count), F32)
    blocks.append(jnp.concatenate(extra + [high, table - high, spare], axis=0))

    ix = positions((SEAM, count))[0]
    even = par_ref[0] == 0
    half = len(blocks) // 2
    for i in range(half):
        one, two = blocks[i], blocks[half + i]
        down = jnp.where(ix == 0, one, roll(two, layer))
        up = jnp.where(ix == 0, roll(one, layer), two)
        rows = slice(i * SEAM, (i + 1) * SEAM)
        a_ref[rows, :] = jnp.where(even, up, down).astype(BF)
        b_ref[rows, :] = jnp.where(even, down, up).astype(BF)


def third_kernel(
    ends_value,
    par_ref,
    inv_ref,
    ext_ref,
    ends_ref,
    table_ref,
    metric_ref,
    emap_ref,
    ra_ref,
    rb_ref,
    refine_ref,
    second_ref,
    lift_x_ref,
    lift_y_ref,
    quad_ref,
    out_ref,
    tmp_ref,
    xs_ref,
    gs_ref,
    vort_ref,
    ws_ref,
    factor_ref,
    normal_x_ref,
    normal_y_ref,
):
    count = ext_ref.shape[-1]
    layer = EY * EZ
    even = par_ref[0] == 0
    ix = positions((SEAM, count))[0]
    end_low, end_high = ends_value

    halves = []
    for i in range(5):
        rows = slice(i * SEAM, (i + 1) * SEAM)
        one = ra_ref[rows, :].astype(F32)
        two = rb_ref[rows, :].astype(F32)
        down = jnp.where(even, two, one)
        up = jnp.where(even, one, two)
        halves.append(
            (
                jnp.where(ix == 0, down, roll(up, layer)),
                jnp.where(ix == 0, roll(down, layer), up),
            )
        )
    blocks = [item[0] for item in halves] + [item[1] for item in halves]

    ix3 = positions((1, 1, count))[0]
    iz24 = positions((HO * HO - 1, count))[2]
    iz1 = positions((1, count))[2]

    def signed(one, two, parity):
        return one + two if parity == 0 else one - two

    def radial(rows, iz, parity):
        last = NI - 1
        low = jnp.where(iz > 0, roll(rows[last], 1) - rows[0], 0.0)
        high = jnp.where(iz < EZ - 1, roll(rows[0], -1) - rows[last], 0.0)
        return [signed(rows[c], rows[last - c], parity) for c in range(HI)] + [
            0.5 * signed(low, high, parity)
        ]

    def stream_added(first, last, halo):
        lane = positions((1,) * (first.ndim - 1) + (count,))[0]
        low = 0.5 * (jnp.where(lane == 0, halo, roll(last, layer)) - first)
        high = 0.5 * (jnp.where(lane == 0, roll(first, -layer), halo) - last)
        return low, high

    seam = {}
    for f in range(7):
        pair, side = PLACE[f]
        lanes = slice(side * count, (side + 1) * count)
        values = ext_ref[f]
        halo = blocks[f].reshape(EXT, NI, count)
        first, last = values[0], values[NI - 1]
        low, high = stream_added(first, last, halo)
        if f in (4, 5):
            seam[f] = seam_rows(jnp.where(ix3 == 0, first + low, last + high))
        for pa in range(2):
            mixed = [signed(values[a], values[NI - 1 - a], pa) for a in range(HI)]
            mixed.append(signed(low, high, pa))
            for pb in range(2):
                at = f % 2 * 4 + pa * 2 + pb
                for a in range(HO):
                    for b in range(HO):
                        one = mixed[a][b if b < HI else NI]
                        two = mixed[a][NI - 1 - b if b < HI else NI + 1]
                        row = (a * HO + b) * NI
                        tmp_ref[at, row : row + NI, :] = signed(one, two, pb)
                main = [tmp_ref[at, pl.ds(c, HO * HO - 1, stride=NI), :] for c in range(NI)]
                start = (HO * HO - 1) * NI
                tail = [tmp_ref[at, start + c : start + c + 1, :] for c in range(NI)]
                for pc in range(2):
                    rows = radial(main, iz24, pc) + radial(tail, iz1, pc)
                    rows.append(jnp.zeros((3, count), F32))
                    operand = jnp.concatenate(rows, axis=0).astype(BF)
                    xs_ref[pair, pa * 4 + pb * 2 + pc, :, lanes] = operand

    def refine(sector, carry):
        for pair in range(4):
            width = 2 * count if pair < 3 else count
            source = xs_ref[pair, sector, :, 0:width]
            source = jnp.concatenate([source, source], axis=0)
            for q, flip in enumerate((0, 4, 2, 1)):
                gs_ref[pair, q, sector ^ flip, :, 0:width] = dot(
                    refine_ref[sector, q * ROWS : (q + 1) * ROWS, :], source
                )
        return carry

    lax.fori_loop(0, 8, refine, 0)

    row = lax.broadcasted_iota(jnp.int32, (ROWS, count), 0)
    a_edge = row < HO * HO
    b_edge = lax.rem(row, HO * HO) < HO
    c_edge = lax.rem(row, HO) == 0

    table = table_ref[...]
    packed = blocks[9]
    theirs = packed[16:40] + packed[40:64]
    lane_ix = positions((24, count))[0]
    at_low = 0.5 * (table + jnp.where(lane_ix == 0, theirs, roll(table, layer)))
    at_high = 0.5 * (table + jnp.where(lane_ix == 0, roll(table, -layer), theirs))

    def line_of(source, at):
        return source[at : at + 1]

    def by_radius(source, at, side):
        return jnp.where(c_edge, line_of(source, at + 1 + side), line_of(source, at))

    for one in range(2):
        edge = at_low if one == 0 else at_high
        for two in range(2):
            at = one * 2 + two
            factor_ref[at] = jnp.where(
                b_edge, by_radius(table, 3 + 3 * one, two), by_radius(table, 0, two)
            )
            factor_ref[4 + at] = jnp.where(
                a_edge, by_radius(edge, 9, two), by_radius(table, 9, two)
            )
            inside = jnp.where(b_edge, line_of(table, 13 + two), line_of(table, 12))
            outside = jnp.where(b_edge, line_of(edge, 13 + two), line_of(edge, 12))
            factor_ref[8 + at] = jnp.where(a_edge, outside, inside)

    def with_added(parts):
        halves = []
        for part in parts:
            stacked = part.reshape(EXT, NI, count)
            halves.append(jnp.concatenate([part, seam_rows(radial_added(stacked))], axis=0))
        operand = jnp.concatenate(halves, axis=1).astype(BF)
        return jnp.concatenate([operand, operand], axis=0)

    stream = []
    for i in range(2):
        shared = jnp.where(ix == 0, end_high, end_low) * seam[4 + i]
        stream.append(blocks[7 + i] + shared)
    lifted = dot(lift_x_ref[...], with_added(stream))
    for one in range(2):
        for two in range(2):
            at = one * 2 + two
            scale = jnp.where(
                b_edge, by_radius(theirs, 3 + 3 * one, two), by_radius(theirs, 0, two)
            )[0:32]
            for i in range(2):
                part = lifted[at * 32 : at * 32 + 32, i * count : (i + 1) * count]
                normal_x_ref[i, at] = part * scale

    iy3 = positions((1, 1, count))[1]
    iy2 = iy3[0]
    azim = []
    for i, f in enumerate((3, 5)):
        factor = jnp.where(iy3 == 0, end_high, end_low)
        values = ext_ref[f]
        halo = blocks[f].reshape(EXT, NI, count)
        near = jnp.where(
            iy3 == 0, values[:, 0] + values[:, NI], values[:, NI - 1] + values[:, NI + 1]
        )
        own = ends_ref[i] + factor * near
        near = jnp.where(iy2 == 0, halo[0] + halo[NI], halo[NI - 1] + halo[NI + 1])
        other = blocks[9][8 * i : 8 * i + 8] + factor[0] * near
        low, high = stream_added(own[0], own[NI - 1], other)
        azim.append(jnp.concatenate([rows2(own), low, high], axis=0))
    lifted = dot(lift_y_ref[...], with_added(azim))
    for one in range(2):
        edge = at_low if one == 0 else at_high
        for two in range(2):
            at = one * 2 + two
            scale = jnp.where(a_edge, by_radius(edge, 15, two), by_radius(table, 15, two))
            for i in range(2):
                part = lifted[at * ROWS : (at + 1) * ROWS, i * count : (i + 1) * count]
                normal_y_ref[i, at] = part * scale

    def nodal(f, q, at):
        pair, side = PLACE[f]
        lanes = slice(side * count, (side + 1) * count)
        return unfold([gs_ref[pair, q, sector, at, lanes] for sector in range(8)])

    everything = slice(0, ROWS)
    lane_ix, lane_iy, lane_iz = positions((ROWS, count))
    wide = slice(0, 32)

    def along_x(i, f):
        g = nodal(f, 1, everything)
        g = [g[s] * factor_ref[s % 4] for s in range(8)]
        near = lane_ix[wide] == 0
        inside = a_edge[wide]
        for at in range(4):
            one, two = g[at][wide], g[4 + at][wide]
            normal = normal_x_ref[i, at]
            first = 0.5 * (one + jnp.where(near, normal, roll(two, layer)))
            last = 0.5 * (two + jnp.where(near, roll(one, -layer), normal))
            g[at] = jnp.concatenate([jnp.where(inside, first, one), g[at][32:]], axis=0)
            g[4 + at] = jnp.concatenate([jnp.where(inside, last, two), g[4 + at][32:]], axis=0)
        return g

    def along_y(i, f):
        g = nodal(f, 2, everything)
        g = [g[s] * factor_ref[4 + s // 4 * 2 + s % 2] for s in range(8)]
        for at in range(4):
            here = at // 2 * 4 + at % 2
            one, two = g[here], g[here + 2]
            normal = normal_y_ref[i, at]
            first = 0.5 * (one + jnp.where(lane_iy == 0, normal, roll(two, EZ)))
            last = 0.5 * (two + jnp.where(lane_iy == EY - 1, normal, roll(one, -EZ)))
            g[here] = jnp.where(b_edge, first, one)
            g[here + 2] = jnp.where(b_edge, last, two)
        return g

    def along_z(f):
        g = nodal(f, 3, everything)
        g = [g[s] * factor_ref[8 + s // 2] for s in range(8)]
        low = c_edge & (lane_iz > 0)
        high = c_edge & (lane_iz < EZ - 1)
        for at in range(4):
            one, two = g[2 * at], g[2 * at + 1]
            g[2 * at] = jnp.where(low, 0.5 * (one + roll(two, 1)), one)
            g[2 * at + 1] = jnp.where(high, 0.5 * (two + roll(one, -1)), two)
        return g

    pairs = (
        (lambda: along_y(1, 5), lambda: along_z(4)),
        (lambda: along_z(3), lambda: along_x(1, 5)),
        (lambda: along_x(0, 4), lambda: along_y(0, 3)),
    )
    uses = {0: ((1, 1), (2, 0)), 1: ((0, 0), (2, 1)), 2: ((0, 1), (1, 0))}
    for i, (plus, minus) in enumerate(pairs):
        one, two = plus(), minus()
        folded = unfold([0.125 * (one[s] - two[s]) for s in range(8)])
        for sector in range(8):
            operand = folded[sector].astype(BF)
            for axis, side in uses[i]:
                vort_ref[axis, sector, :, side * count : (side + 1) * count] = operand

    for axis in range(3):
        flip = (4, 2, 1)[axis]
        for sector in range(8):
            source = vort_ref[axis, sector]
            source = jnp.concatenate([source, source], axis=0)
            which = 2 * axis + (1 if sector & flip else 0)
            ws_ref[axis, sector ^ flip] = dot(second_ref[which], source)

    metric = [metric_ref[i : i + 1] for i in range(3)]
    inv = inv_ref[0]
    scaled = [inv * metric[i] for i in range(3)]

    def body(step, total):
        at = pl.ds(pl.multiple_of(step * 8, 8), 8)
        for side in range(2):
            total = total + quad_ref[at, :] * energy_of(at, side)
        return total

    def energy_of(at, side):
        def unfold_half(parts):
            return unfold4([signed(parts[s], parts[4 + s], side) for s in range(4)])

        def part(f, q):
            pair, half = PLACE[f]
            lanes = slice(half * count, (half + 1) * count)
            return unfold_half([gs_ref[pair, q, s, at, lanes] for s in range(8)])

        def curl(axis, half, sector):
            return ws_ref[axis, sector, at, half * count : (half + 1) * count]

        base = [[item * metric[j] for item in part(j, 0)] for j in range(3)]
        dual = [part(3 + j, 0) for j in range(3)]
        energy = spread = None
        terms = (((1, 0), (2, 1)), ((2, 0), (0, 1)), ((0, 0), (1, 1)))
        for i in range(3):
            plus, minus = terms[i]
            linear = []
            for s in range(8):
                viscous = scaled[plus[0]] * curl(plus[0], plus[1], s)
                viscous = viscous - scaled[minus[0]] * curl(minus[0], minus[1], s)
                linear.append(gs_ref[1, 1 + i, s, at, count : 2 * count] * metric[i] + viscous)
            total = unfold_half(linear)
            for j in range(3):
                slope = part(3 + i, 1 + j)
                total = [total[s] - base[j][s] * slope[s] for s in range(4)]
                if i == j:
                    more = [slope[s] * metric[i] for s in range(4)]
                    spread = more if i == 0 else [spread[s] + more[s] for s in range(4)]
            inner = None
            for j in range(3):
                slope = part(j, 1 + i)
                more = [dual[j][s] * slope[s] for s in range(4)]
                inner = more if j == 0 else [inner[s] + more[s] for s in range(4)]
            total = [total[s] + metric[i] * inner[s] for s in range(4)]
            more = [item * item for item in total]
            energy = more if i == 0 else [energy[s] + more[s] for s in range(4)]
        energy = [energy[s] + spread[s] * spread[s] for s in range(4)]
        return (energy[0] + energy[1]) + (energy[2] + energy[3])

    total = lax.fori_loop(0, ROWS // 8, body, jnp.zeros((8, count), F32))
    weighted = jnp.sum(total, axis=0, keepdims=True)
    result = jnp.sqrt(weighted / 8.0) / float(ORDER_OUT**2)
    high, mid, low = split3(result)
    stacked = jnp.concatenate(
        [high.astype(F32), mid.astype(F32), low.astype(F32), jnp.zeros((13, count), F32)], axis=0
    )
    moved = dot(stacked.astype(BF), slot_matrix(emap_ref, count))
    out_ref[...] = moved[0:1] + moved[1:2] + moved[2:3]


def unfold4(parts):
    plus0, minus0 = parts[0] + parts[1], parts[0] - parts[1]
    plus1, minus1 = parts[2] + parts[3], parts[2] - parts[3]
    return [plus0 + plus1, minus0 + minus1, plus0 - plus1, minus0 - minus1]


def unfold(parts):
    plus = unfold4([parts[s] + parts[4 + s] for s in range(4)])
    minus = unfold4([parts[s] - parts[4 + s] for s in range(4)])
    return plus + minus


LIMIT = 60 * 1024 * 1024


def per_device(fields, elem_map, metric, inv_reynolds):
    refine, second, lift_x, lift_y, quad, (line, ends_value) = tables()
    count = fields.shape[-1]
    vmem = pl.BlockSpec(memory_space=pltpu.VMEM)
    smem = pl.BlockSpec(memory_space=pltpu.SMEM)
    params = pltpu.CompilerParams(vmem_limit_bytes=LIMIT)

    def struct(shape, dtype=F32):
        return jax.ShapeDtypeStruct(shape, dtype)

    coarse, local_metric, message = pl.pallas_call(
        functools.partial(first_kernel, line),
        out_shape=(
            struct((7, NI, NI, NI, count)),
            struct((8, count)),
            struct((9 * 64 + 16, count), BF),
        ),
        in_specs=[vmem] * 3,
        out_specs=(vmem,) * 3,
        compiler_params=params,
        name="first",
    )(fields, elem_map, metric)

    azim = lax.axis_size("azim")
    if azim == 2:
        halo = lax.ppermute(message, "azim", [(0, 1), (1, 0)])
    else:
        ahead = lax.ppermute(message, "azim", [(i, (i + 1) % azim) for i in range(azim)])
        behind = lax.ppermute(message, "azim", [((i + 1) % azim, i) for i in range(azim)])
        iy = (jnp.arange(count) // EZ) % EY
        halo = jnp.where(iy >= EY // 2, ahead, behind)

    place = lax.axis_index("strm")
    streams = lax.axis_size("strm")
    parity = lax.rem(place, 2).astype(jnp.int32).reshape(1)
    if streams % 2:
        parity = jnp.zeros((1,), jnp.int32)
    extended, ends, table, to_a, to_b = pl.pallas_call(
        functools.partial(second_kernel, line),
        out_shape=(
            struct((7, NI, EXT, NI, count)),
            struct((2, NI, NI, count)),
            struct((24, count)),
            struct((5 * SEAM, count), BF),
            struct((5 * SEAM, count), BF),
        ),
        in_specs=[smem] + [vmem] * 3,
        out_specs=(vmem,) * 5,
        compiler_params=params,
        name="second",
    )(parity, coarse, local_metric, halo)

    if streams % 2 == 0:
        near = [(i, i ^ 1) for i in range(streams)]
        far = []
        for i in range(1, streams, 2):
            far += [(i, (i + 1) % streams), ((i + 1) % streams, i)]
        got_a = lax.ppermute(to_a, "strm", near)
        got_b = lax.ppermute(to_b, "strm", far)
    else:
        got_b = lax.ppermute(to_a, "strm", [(i, (i + 1) % streams) for i in range(streams)])
        got_a = lax.ppermute(to_b, "strm", [((i + 1) % streams, i) for i in range(streams)])

    result = pl.pallas_call(
        functools.partial(third_kernel, ends_value),
        out_shape=struct((1, count)),
        in_specs=[smem] * 2 + [vmem] * 12,
        out_specs=vmem,
        scratch_shapes=[
            pltpu.VMEM((8, HO * HO * NI, count), F32),
            pltpu.VMEM((4, 8, ROWS, 2 * count), BF),
            pltpu.VMEM((4, 4, 8, ROWS, 2 * count), F32),
            pltpu.VMEM((3, 8, ROWS, 2 * count), BF),
            pltpu.VMEM((3, 8, ROWS, 2 * count), F32),
            pltpu.VMEM((12, ROWS, count), F32),
            pltpu.VMEM((2, 4, 32, count), F32),
            pltpu.VMEM((2, 4, ROWS, count), F32),
        ],
        compiler_params=params,
        name="third",
    )(
        parity,
        inv_reynolds,
        extended,
        ends,
        table,
        local_metric,
        elem_map,
        got_a,
        got_b,
        jnp.asarray(refine),
        jnp.asarray(second),
        jnp.asarray(lift_x),
        jnp.asarray(lift_y),
        jnp.asarray(quad),
    )
    return result.reshape(count)


def solution(mesh):
    return jax.shard_map(
        per_device,
        mesh=mesh,
        in_specs=(
            P(None, None, ("grp", "strm", "azim")),
            P(("strm", "azim"), None),
            P(None, ("strm", "azim")),
            P("grp"),
        ),
        out_specs=P(("grp", "strm", "azim")),
        check_vma=False,
    )
```

profile of v0, /device:TPU:0, one launch (start us, length us, event | category | flops | bytes accessed | tf_op | source)
XLA Modules:
  0.0 33.5 jit_solution(6453092742720238398)
XLA Ops:
  0.0 2.9 %first.1 = (f32[7,8,8,8,128]{4,3,2,1,0:T(8,128)}, f32[8,128]{1,0:T(8,128)}, bf16[592,128]{1,0:T(8,128)(2,1)}) custom-call(bf16[7,512,128]{2,1,0:T(8,128)(2,1)} %fields_ref.1, s32[1,128]{1,0:T(1,128)} %emap_ref.3, f32[3,128]{1,0:T(4,128)} %metric_ref.1), custom_call_target="tpu_custom_call" | custom-call | tf_op jit(solution)/shard_map/first/pallas_call | solution.py:673
  2.9 0.5 %collective-permute-start = (bf16[592,128]{1,0:T(8,128)(2,1)}, bf16[592,128]{1,0:T(8,128)(2,1)S(1)}, u32[]{:S(2)}, u32[]{:S(2)}) collective-permute-start(bf16[592,128]{1,0:T(8,128)(2,1)} %get-tuple-element.15), channel_id=1, source_target_pairs={{0,1},{1,0},{2,3},{3,2},{4,5},{5,4},{6,7},{7,6},{8,9},{9,8},{10,11... | collective-permute-start | bytes 454664 | tf_op jit(solution)/shard_map/ppermute | solution.py:688
  3.4 1.2 %collective-permute-done.halo_ref = bf16[592,128]{1,0:T(8,128)(2,1)S(1)} collective-permute-done((bf16[592,128]{1,0:T(8,128)(2,1)}, bf16[592,128]{1,0:T(8,128)(2,1)S(1)}, u32[]{:S(2)}, u32[]{:S(2)}) %collective-permute-start) | collective-permute-done | bytes 151584 | tf_op jit(solution)/shard_map/ppermute | solution.py:688
  4.6 0.0 copy-start
  4.6 0.6 %copy-done = bf16[592,128]{1,0:T(8,128)(2,1)} copy-done((bf16[592,128]{1,0:T(8,128)(2,1)}, bf16[592,128]{1,0:T(8,128)(2,1)S(1)}, u32[]{:S(2)}) %copy-start) | copy-done | bytes 151576
  5.3 3.5 %second.1 = (f32[7,8,10,8,128]{4,3,2,1,0:T(8,128)}, f32[2,8,8,128]{3,2,1,0:T(8,128)}, f32[24,128]{1,0:T(8,128)}, bf16[400,128]{1,0:T(8,128)(2,1)}, bf16[400,128]{1,0:T(8,128)(2,1)}) custom-call(s32[1]{0:T(128)} %bitcast.par_ref, f32[7,8,8,8,128]{4,3,2,1,0:T(8,128)} %get-tuple-element.13.coarse_ref, f32[8,128]{1,0:T(8,128)} %get-tuple-element.14.metric_ref, ...), custom_call_target="tpu_custom_call" | custom-call | tf_op jit(solution)/shard_map/second/pallas_call | solution.py:700
  8.8 2.8 %collective-permute-start.1 = (bf16[400,128]{1,0:T(8,128)(2,1)}, bf16[400,128]{1,0:T(8,128)(2,1)S(1)}, u32[]{:S(2)}, u32[]{:S(2)}) collective-permute-start(bf16[400,128]{1,0:T(8,128)(2,1)} %get-tuple-element.19), channel_id=1, source_target_pairs={{0,2},{2,0},{4,6},{6,4},{8,10},{10,8},{12,14},{14,12},{1,3},{3,1},... | collective-permute-start | bytes 307208 | tf_op jit(solution)/shard_map/ppermute | solution.py:720
  11.6 3.6 %collective-permute-start.2 = (bf16[400,128]{1,0:T(8,128)(2,1)}, bf16[400,128]{1,0:T(8,128)(2,1)S(1)}, u32[]{:S(2)}, u32[]{:S(2)}) collective-permute-start(bf16[400,128]{1,0:T(8,128)(2,1)} %get-tuple-element.20), channel_id=1, source_target_pairs={{2,4},{4,2},{6,8},{8,6},{10,12},{12,10},{14,0},{0,14},{3,5},{5,3},... | collective-permute-start | bytes 307208 | tf_op jit(solution)/shard_map/ppermute | solution.py:721
  15.8 0.7 %collective-permute-done.1.ra_ref = bf16[400,128]{1,0:T(8,128)(2,1)S(1)} collective-permute-done((bf16[400,128]{1,0:T(8,128)(2,1)}, bf16[400,128]{1,0:T(8,128)(2,1)S(1)}, u32[]{:S(2)}, u32[]{:S(2)}) %collective-permute-start.1) | collective-permute-done | bytes 102432 | tf_op jit(solution)/shard_map/ppermute | solution.py:720
  16.6 0.0 copy-start.1
  16.6 2.6 %collective-permute-done.2.rb_ref = bf16[400,128]{1,0:T(8,128)(2,1)S(1)} collective-permute-done((bf16[400,128]{1,0:T(8,128)(2,1)}, bf16[400,128]{1,0:T(8,128)(2,1)S(1)}, u32[]{:S(2)}, u32[]{:S(2)}) %collective-permute-start.2) | collective-permute-done | bytes 102432 | tf_op jit(solution)/shard_map/ppermute | solution.py:721
  19.2 0.0 copy-start.2
  19.2 0.0 copy-done.1
  19.2 0.6 %copy-done.2 = bf16[400,128]{1,0:T(8,128)(2,1)} copy-done((bf16[400,128]{1,0:T(8,128)(2,1)}, bf16[400,128]{1,0:T(8,128)(2,1)S(1)}, u32[]{:S(2)}) %copy-start.2) | copy-done | bytes 102424
  19.9 13.6 %third.1 = f32[1,128]{1,0:T(1,128)} custom-call(s32[1]{0:T(128)} %bitcast.par_ref, f32[1]{0:T(128)S(6)} %copy.10.inv_ref, f32[7,8,10,8,128]{4,3,2,1,0:T(8,128)} %get-tuple-element.16.ext_ref, f32[2,8,8,128]{3,2,1,0:T(8,128)} %get-tuple-element.17.ends_ref, f32[24,128]{1,0:T(8,128)} %get-tuple-element.18.table_ref, f32[8,128]{1,0:T(8,128)} %get-tuple-element.14.metric_ref, ...), custom_call_target="tpu_custom_call" | custom-call | tf_op jit(solution)/shard_map/third/pallas_call | solution.py:726
Async XLA Ops:
  2.9 1.7 %collective-permute-start = (bf16[592,128]{1,0:T(8,128)(2,1)}, bf16[592,128]{1,0:T(8,128)(2,1)S(1)}, u32[]{:S(2)}, u32[]{:S(2)}) collective-permute-start(bf16[592,128]{1,0:T(8,128)(2,1)} %get-tuple-element.15), channel_id=1, source_target_pairs={{0,1},{1,0},{2,3},{3,2},{4,5},{5,4},{6,7},{7,6},{8,9},{9,8},{10,11... | collective-permute-start | bytes 454664 | tf_op jit(solution)/shard_map/ppermute | solution.py:688
  4.6 0.6 %copy-start = (bf16[592,128]{1,0:T(8,128)(2,1)}, bf16[592,128]{1,0:T(8,128)(2,1)S(1)}, u32[]{:S(2)}) copy-start(bf16[592,128]{1,0:T(8,128)(2,1)S(1)} %collective-permute-done.halo_ref) | copy-start | bytes 454660
  8.8 7.8 %collective-permute-start.1 = (bf16[400,128]{1,0:T(8,128)(2,1)}, bf16[400,128]{1,0:T(8,128)(2,1)S(1)}, u32[]{:S(2)}, u32[]{:S(2)}) collective-permute-start(bf16[400,128]{1,0:T(8,128)(2,1)} %get-tuple-element.19), channel_id=1, source_target_pairs={{0,2},{2,0},{4,6},{6,4},{8,10},{10,8},{12,14},{14,12},{1,3},{3,1},... | collective-permute-start | bytes 307208 | tf_op jit(solution)/shard_map/ppermute | solution.py:720
  11.6 7.6 %collective-permute-start.2 = (bf16[400,128]{1,0:T(8,128)(2,1)}, bf16[400,128]{1,0:T(8,128)(2,1)S(1)}, u32[]{:S(2)}, u32[]{:S(2)}) collective-permute-start(bf16[400,128]{1,0:T(8,128)(2,1)} %get-tuple-element.20), channel_id=1, source_target_pairs={{2,4},{4,2},{6,8},{8,6},{10,12},{12,10},{14,0},{0,14},{3,5},{5,3},... | collective-permute-start | bytes 307208 | tf_op jit(solution)/shard_map/ppermute | solution.py:721
  16.6 2.6 %copy-start.1 = (bf16[400,128]{1,0:T(8,128)(2,1)}, bf16[400,128]{1,0:T(8,128)(2,1)S(1)}, u32[]{:S(2)}) copy-start(bf16[400,128]{1,0:T(8,128)(2,1)S(1)} %collective-permute-done.1.ra_ref) | copy-start | bytes 307204
  19.2 0.7 %copy-start.2 = (bf16[400,128]{1,0:T(8,128)(2,1)}, bf16[400,128]{1,0:T(8,128)(2,1)S(1)}, u32[]{:S(2)}) copy-start(bf16[400,128]{1,0:T(8,128)(2,1)S(1)} %collective-permute-done.2.rb_ref) | copy-start | bytes 307204
where the time goes:
time: 33.6 us; the launch traced here: 33.5 us
  Pallas kernels  20 us (60%)
  starting transfers between devices  6.9 us (21%)
  waiting for transfers between devices  4.57 us (14%)
  local copies, waits for them, and re-layouts  1.3 us (4%)
  between operations  0.66 us (2%)
    pallas_call x1, Pallas kernels, per_device(): pl.pallas_call(functools.partial(third_kernel, ends_value), out_shape=str...  13.6 us
    ppermute x1, starting transfers between devices, per_device(): got_b = lax.ppermute(to_b, 'strm', far)  3.57 us
    pallas_call x1, Pallas kernels, per_device(): pl.pallas_call(functools.partial(second_kernel, line), out_shape=(struct(...  3.53 us
    pallas_call x1, Pallas kernels, per_device(): pl.pallas_call(functools.partial(first_kernel, line), out_shape=(struct((...  2.89 us
    ppermute x1, starting transfers between devices, per_device(): got_a = lax.ppermute(to_a, 'strm', near)  2.84 us
    ppermute x1, waiting for transfers between devices, per_device(): got_b = lax.ppermute(to_b, 'strm', far)  2.6 us
    unnamed x6, local copies, waits for them, and re-layouts  1.3 us
    ppermute x1, waiting for transfers between devices, per_device(): halo = lax.ppermute(message, 'azim', [(0, 1), (1, 0)])  1.22 us
  transfers between devices with their start and end apart: 3, of which 3 were waited for; matrix products, arithmetic and copies ran while one was open for 0% of the time, Pallas kernels for 0%

commit v1 on v0

--- a/solution.py
+++ b/solution.py
@@ -17,11 +17,14 @@
 HI = NI // 2
 HO = NO // 2
 ROWS = 128
+SEAM_ROWS = ROWS + 3 * 32
 EXT = NI + 2
 SEAM = EXT * NI
 BF = jnp.bfloat16
 F32 = jnp.float32
-PLACE = {3: (0, 0), 4: (0, 1), 5: (1, 0), 6: (1, 1), 0: (2, 0), 1: (2, 1), 2: (3, 0)}
+PLACE = {3: (0, 0), 4: (0, 1), 5: (1, 0), 0: (1, 1), 1: (2, 0), 2: (2, 1), 6: (3, 0)}
+PAIRS = 4
+FLIPS = (0, 4, 2, 1)
 
 
 def gll_table(extent):
@@ -100,10 +103,10 @@
             right = matrix[:HO, ::-1][:, :HO]
         return left + sign * right
 
-    refine = []
+    refine, seams = [], []
     for sector in range(8):
         pa, pb, pc = sector // 4, sector // 2 % 2, sector % 2
-        blocks = []
+        blocks, ends_of = [], []
         for ta, tb, tc in (
             (value, value, value),
             (both, value, value),
@@ -112,12 +115,20 @@
         ):
             block = 0.125 * np.einsum(
                 "ap,bq,cr->abcrpq", folded(ta, pa), folded(tb, pb), folded(tc, pc)
-            ).reshape(HO**3, HO, HO * HO)
-            main = block[:, :, : HO * HO - 1].reshape(HO**3, -1)
-            tail = np.pad(block[:, :, HO * HO - 1], ((0, 0), (0, ROWS - main.shape[1] - HO)))
-            blocks.append(pad_rows(np.concatenate([main, tail], axis=1), ROWS))
+            ).reshape(HO**3, HO, HO, HO)
+            own = np.zeros((HO**3, HO, 24))
+            own[:, :, : HO * HI] = block[:, :, :HI].reshape(HO**3, HO, HO * HI)
+            own = np.pad(own.reshape(HO**3, -1), ((0, 0), (0, ROWS - 24 * HO)))
+            blocks.append(pad_rows(own, ROWS))
+            added = np.zeros((HO**3, 48))
+            added[:, : 8 * HO] = np.pad(block[:, :, HI], ((0, 0), (0, 0), (0, 3))).reshape(HO**3, -1)
+            ends_of.append(added)
         refine.append(two_terms(np.concatenate(blocks)))
+        rows = [pad_rows(ends_of[1], ROWS)]
+        rows += [pad_rows(ends_of[q][: HO * HO], 32) for q in (0, 2, 3)]
+        seams.append(np.pad(two_terms(np.concatenate(rows)), ((0, 0), (0, ROWS - 96))))
     refine = np.stack(refine)
+    seams = [np.concatenate(seams[2 * i : 2 * i + 2], axis=1) for i in range(4)]
 
     second = []
     eye = np.eye(HO)
@@ -146,19 +157,24 @@
             spread = np.zeros((HO, HO, HO, 2 * SEAM))
             spread[:, 0] = face
             lift_y.append(pad_rows(spread.reshape(HO**3, -1), ROWS))
-    lift_x = two_terms(np.concatenate(lift_x))
-    lift_y = two_terms(np.concatenate(lift_y))
-
-    half_weights = weights[:HO]
-    quad = np.kron(np.kron(half_weights, half_weights), half_weights)[:, None]
-    quad = np.broadcast_to(pad_rows(quad, ROWS), (ROWS, 128)).astype(np.float32)
+
+    def one_term(parts):
+        matrix = np.concatenate(parts)
+        return np.pad(matrix, ((0, 0), (0, 2 * ROWS - matrix.shape[1]))).astype(jnp.bfloat16)
+
+    const = np.concatenate(
+        [refine.reshape(-1, 2 * ROWS)]
+        + seams
+        + [second.reshape(-1, 2 * ROWS), one_term(lift_x), one_term(lift_y)]
+    )
+    half_weights = [float(v) for v in weights[:HO]]
     line = []
     for end, far in ((0, NO - 1), (NO - 1, 0)):
         weights_in = slopes[end].copy()
         weights_in[[0, NO - 1]] = 0.0
         line.append(([float(v) for v in weights_in @ interp], float(slopes[end, far])))
     ends = (float(slopes[0, 0]), float(slopes[NO - 1, NO - 1]))
-    return refine, second, lift_x, lift_y, quad, (line, ends)
+    return const, half_weights, (line, ends)
 
 
 def dot(a, b, contract_last=False):
@@ -194,11 +210,6 @@
     mid = rest.astype(BF)
     low = (rest - mid.astype(F32)).astype(BF)
     return high, mid, low
-
-
-def slot_matrix(emap_ref, count):
-    local = lax.broadcasted_iota(jnp.int32, (count, count), 0)
-    return (local == emap_ref[...]).astype(F32).astype(BF)
 
 
 def radial_added(x):
@@ -226,10 +237,12 @@
     return one, two
 
 
-def first_kernel(line, fields_ref, emap_ref, metric_ref, coarse_ref, metric_out, msg_ref):
-    count = fields_ref.shape[-1]
-    slots = slot_matrix(emap_ref, count)
-    high, mid, low = split3(metric_ref[...])
+def first_kernel(line, fields, small_ref, slots_ref, metric_out, msg_ref):
+    count = fields.shape[-1]
+    local = lax.broadcasted_iota(jnp.int32, (count, count), 0).astype(F32)
+    slots = (local == small_ref[0:1]).astype(F32).astype(BF)
+    slots_ref[...] = slots
+    high, mid, low = split3(small_ref[1:4])
     pad = jnp.zeros((7, count), F32)
     stacked = jnp.concatenate([high.astype(F32), mid.astype(F32), low.astype(F32), pad], axis=0)
     moved = dot(stacked.astype(BF), slots, True)
@@ -240,14 +253,20 @@
     msg_ref[9 * 64 : 9 * 64 + 16, :] = tail.astype(BF)
     iy = positions((1, 1, count))[1]
     for f in range(7):
-        values = dot(fields_ref[f], slots, True).reshape(NI, NI, NI, count)
-        coarse_ref[f] = values
+        values = dot(fields[f], slots, True).reshape(NI, NI, NI, count)
         face = jnp.where(iy == 0, values[:, 0], values[:, NI - 1])
         msg_ref[f * 64 : f * 64 + 64, :] = rows2(face).astype(BF)
         if f in (3, 5):
             low, high = end_lines(line, [values[:, b] for b in range(NI)], EZ)
             at = (7 + (f == 5)) * 64
             msg_ref[at : at + 64, :] = rows2(jnp.where(iy == 0, low, high)).astype(BF)
+
+
+def own_kernel(fields_ref, slots_ref, coarse_ref):
+    count = fields_ref.shape[-1]
+    for f in range(7):
+        values = dot(fields_ref[f], slots_ref[...], True)
+        coarse_ref[f] = values.reshape(NI, NI, NI, count)
 
 
 def from_azim(x, iy):
@@ -323,37 +342,102 @@
         b_ref[rows, :] = jnp.where(even, down, up).astype(BF)
 
 
-def third_kernel(
+def signed(one, two, parity):
+    return one + two if parity == 0 else one - two
+
+
+def radial_fold(rows, iz, parity):
+    last = NI - 1
+    low = jnp.where(iz > 0, roll(rows[last], 1) - rows[0], 0.0)
+    high = jnp.where(iz < EZ - 1, roll(rows[0], -1) - rows[last], 0.0)
+    return [signed(rows[c], rows[last - c], parity) for c in range(HI)] + [
+        0.5 * signed(low, high, parity)
+    ]
+
+
+def azim_fold(plane, parity):
+    return [
+        signed(
+            plane[b if b < HI else NI], plane[NI - 1 - b if b < HI else NI + 1], parity
+        )
+        for b in range(HO)
+    ]
+
+
+def third_kernel(ext_ref, const_ref, gs_ref, tmp_ref, xs_ref):
+    count = ext_ref.shape[-1]
+    width = HO * HI
+    iz = positions((width, count))[2]
+    zeros = jnp.zeros((HI, count), F32)
+    for f in range(7):
+        pair, side = PLACE[f]
+        lanes = slice(side * count, (side + 1) * count)
+        values = ext_ref[f]
+        for pa in range(2):
+            mixed = [signed(values[a], values[NI - 1 - a], pa) for a in range(HI)]
+            for pb in range(2):
+                at = f % 2 * 4 + pa * 2 + pb
+                for a in range(HI):
+                    for b, item in enumerate(azim_fold(mixed[a], pb)):
+                        row = (a * HO + b) * NI
+                        tmp_ref[at, row : row + NI, :] = item
+                main = [tmp_ref[at, pl.ds(c, width, stride=NI), :] for c in range(NI)]
+                for pc in range(2):
+                    rows = []
+                    for item in radial_fold(main, iz, pc):
+                        rows += [item, zeros]
+                    rows.append(jnp.zeros((8, count), F32))
+                    operand = jnp.concatenate(rows, axis=0).astype(BF)
+                    xs_ref[pair, pa * 4 + pb * 2 + pc, :, lanes] = operand
+
+    def refine(sector, carry):
+        for pair in range(PAIRS):
+            width = 2 * count if pair < PAIRS - 1 else count
+            source = xs_ref[pair, sector, :, 0:width]
+            source = jnp.concatenate([source, source], axis=0)
+            for q in range(0 if pair < PAIRS - 1 else 1, 4):
+                rows = pl.ds(sector * 4 * ROWS + q * ROWS, ROWS)
+                gs_ref[pair, q, sector ^ FLIPS[q], :, 0:width] = dot(const_ref[rows, :], source)
+        return carry
+
+    lax.fori_loop(0, 8, refine, 0)
+
+
+def fourth_kernel(
     ends_value,
+    weights,
     par_ref,
     inv_ref,
+    gs_ref,
     ext_ref,
     ends_ref,
     table_ref,
     metric_ref,
-    emap_ref,
+    slots_ref,
     ra_ref,
     rb_ref,
-    refine_ref,
-    second_ref,
-    lift_x_ref,
-    lift_y_ref,
-    quad_ref,
+    const_ref,
     out_ref,
     tmp_ref,
-    xs_ref,
-    gs_ref,
+    along_ref,
+    edge_ref,
     vort_ref,
-    ws_ref,
+    linear_ref,
     factor_ref,
     normal_x_ref,
     normal_y_ref,
+    quad_ref,
+    xt_ref,
 ):
     count = ext_ref.shape[-1]
     layer = EY * EZ
     even = par_ref[0] == 0
     ix = positions((SEAM, count))[0]
     end_low, end_high = ends_value
+    seam_at = 8 * 4 * ROWS
+    second_at = seam_at + 4 * SEAM_ROWS
+    lift_x_at = second_at + 6 * ROWS
+    lift_y_at = lift_x_at + ROWS
 
     halves = []
     for i in range(5):
@@ -371,19 +455,7 @@
     blocks = [item[0] for item in halves] + [item[1] for item in halves]
 
     ix3 = positions((1, 1, count))[0]
-    iz24 = positions((HO * HO - 1, count))[2]
-    iz1 = positions((1, count))[2]
-
-    def signed(one, two, parity):
-        return one + two if parity == 0 else one - two
-
-    def radial(rows, iz, parity):
-        last = NI - 1
-        low = jnp.where(iz > 0, roll(rows[last], 1) - rows[0], 0.0)
-        high = jnp.where(iz < EZ - 1, roll(rows[0], -1) - rows[last], 0.0)
-        return [signed(rows[c], rows[last - c], parity) for c in range(HI)] + [
-            0.5 * signed(low, high, parity)
-        ]
+    iz8 = positions((NI, count))[2]
 
     def stream_added(first, last, halo):
         lane = positions((1,) * (first.ndim - 1) + (count,))[0]
@@ -392,52 +464,65 @@
         return low, high
 
     seam = {}
+    tmp_ref[...] = jnp.zeros(tmp_ref.shape, F32)
     for f in range(7):
         pair, side = PLACE[f]
         lanes = slice(side * count, (side + 1) * count)
-        values = ext_ref[f]
         halo = blocks[f].reshape(EXT, NI, count)
-        first, last = values[0], values[NI - 1]
+        first, last = ext_ref[f, 0], ext_ref[f, NI - 1]
         low, high = stream_added(first, last, halo)
         if f in (4, 5):
             seam[f] = seam_rows(jnp.where(ix3 == 0, first + low, last + high))
         for pa in range(2):
-            mixed = [signed(values[a], values[NI - 1 - a], pa) for a in range(HI)]
-            mixed.append(signed(low, high, pa))
+            mixed = signed(low, high, pa)
             for pb in range(2):
                 at = f % 2 * 4 + pa * 2 + pb
-                for a in range(HO):
-                    for b in range(HO):
-                        one = mixed[a][b if b < HI else NI]
-                        two = mixed[a][NI - 1 - b if b < HI else NI + 1]
-                        row = (a * HO + b) * NI
-                        tmp_ref[at, row : row + NI, :] = signed(one, two, pb)
-                main = [tmp_ref[at, pl.ds(c, HO * HO - 1, stride=NI), :] for c in range(NI)]
-                start = (HO * HO - 1) * NI
-                tail = [tmp_ref[at, start + c : start + c + 1, :] for c in range(NI)]
+                for b, item in enumerate(azim_fold(mixed, pb)):
+                    tmp_ref[at, b * NI : (b + 1) * NI, :] = item
+                main = [tmp_ref[at, pl.ds(c, NI, stride=NI), :] for c in range(NI)]
                 for pc in range(2):
-                    rows = radial(main, iz24, pc) + radial(tail, iz1, pc)
-                    rows.append(jnp.zeros((3, count), F32))
+                    rows = radial_fold(main, iz8, pc)
+                    rows.append(jnp.zeros((NI, count), F32))
                     operand = jnp.concatenate(rows, axis=0).astype(BF)
-                    xs_ref[pair, pa * 4 + pb * 2 + pc, :, lanes] = operand
-
-    def refine(sector, carry):
-        for pair in range(4):
-            width = 2 * count if pair < 3 else count
-            source = xs_ref[pair, sector, :, 0:width]
-            source = jnp.concatenate([source, source], axis=0)
-            for q, flip in enumerate((0, 4, 2, 1)):
-                gs_ref[pair, q, sector ^ flip, :, 0:width] = dot(
-                    refine_ref[sector, q * ROWS : (q + 1) * ROWS, :], source
-                )
-        return carry
-
-    lax.fori_loop(0, 8, refine, 0)
+                    xt_ref[pair, pa * 4 + pb * 2 + pc, :, lanes] = operand
+
+    def refine_seam(pa, pb, pc):
+        sector = pa * 4 + pb * 2 + pc
+        at = seam_at + (sector // 2) * SEAM_ROWS
+        matrix = const_ref[at : at + SEAM_ROWS, pc * ROWS : pc * ROWS + 2 * 48]
+        for pair in range(PAIRS):
+            width = 2 * count if pair < PAIRS - 1 else count
+            source = xt_ref[pair, sector, :, 0:width]
+            added = dot(matrix, jnp.concatenate([source, source], axis=0))
+            target = sector ^ 4
+            along_ref[pair, target, :, 0:width] = (
+                gs_ref[pair, 1, target, :, 0:width] + added[0:ROWS]
+            )
+            for q, slot in ((0, 0), (2, 1), (3, 2)):
+                if q or pair < PAIRS - 1:
+                    target = sector ^ FLIPS[q]
+                    edge_ref[pair, slot, target, :, 0:width] = (
+                        gs_ref[pair, q, target, 0:32, 0:width]
+                        + added[ROWS + 32 * slot : ROWS + 32 * slot + 32]
+                    )
+
+    for sector in range(8):
+        refine_seam(sector // 4, sector // 2 % 2, sector % 2)
 
     row = lax.broadcasted_iota(jnp.int32, (ROWS, count), 0)
     a_edge = row < HO * HO
     b_edge = lax.rem(row, HO * HO) < HO
     c_edge = lax.rem(row, HO) == 0
+
+    def weight_of(index):
+        result = jnp.full((ROWS, count), weights[0], F32)
+        for i in range(1, HO):
+            result = jnp.where(index == i, weights[i], result)
+        return result
+
+    a_pos = lax.div(row, HO * HO)
+    quad = weight_of(a_pos) * weight_of(lax.rem(lax.div(row, HO), HO)) * weight_of(lax.rem(row, HO))
+    quad_ref[...] = jnp.where(row < HO**3, quad, 0.0)
 
     table = table_ref[...]
     packed = blocks[9]
@@ -471,14 +556,16 @@
         for part in parts:
             stacked = part.reshape(EXT, NI, count)
             halves.append(jnp.concatenate([part, seam_rows(radial_added(stacked))], axis=0))
-        operand = jnp.concatenate(halves, axis=1).astype(BF)
-        return jnp.concatenate([operand, operand], axis=0)
+        return jnp.concatenate(halves, axis=1).astype(BF)
+
+    def lift(at, rows, operand):
+        return dot(const_ref[at : at + rows, 0 : 2 * SEAM], operand)
 
     stream = []
     for i in range(2):
         shared = jnp.where(ix == 0, end_high, end_low) * seam[4 + i]
         stream.append(blocks[7 + i] + shared)
-    lifted = dot(lift_x_ref[...], with_added(stream))
+    lifted = lift(lift_x_at, ROWS, with_added(stream))
     for one in range(2):
         for two in range(2):
             at = one * 2 + two
@@ -504,7 +591,7 @@
         other = blocks[9][8 * i : 8 * i + 8] + factor[0] * near
         low, high = stream_added(own[0], own[NI - 1], other)
         azim.append(jnp.concatenate([rows2(own), low, high], axis=0))
-    lifted = dot(lift_y_ref[...], with_added(azim))
+    lifted = lift(lift_y_at, 4 * ROWS, with_added(azim))
     for one in range(2):
         edge = at_low if one == 0 else at_high
         for two in range(2):
@@ -514,109 +601,130 @@
                 part = lifted[at * ROWS : (at + 1) * ROWS, i * count : (i + 1) * count]
                 normal_y_ref[i, at] = part * scale
 
-    def nodal(f, q, at):
+    def parts_of(f, q, at, edge):
         pair, side = PLACE[f]
         lanes = slice(side * count, (side + 1) * count)
-        return unfold([gs_ref[pair, q, sector, at, lanes] for sector in range(8)])
-
-    everything = slice(0, ROWS)
-    lane_ix, lane_iy, lane_iz = positions((ROWS, count))
-    wide = slice(0, 32)
-
-    def along_x(i, f):
-        g = nodal(f, 1, everything)
-        g = [g[s] * factor_ref[s % 4] for s in range(8)]
-        near = lane_ix[wide] == 0
-        inside = a_edge[wide]
-        for at in range(4):
-            one, two = g[at][wide], g[4 + at][wide]
-            normal = normal_x_ref[i, at]
-            first = 0.5 * (one + jnp.where(near, normal, roll(two, layer)))
-            last = 0.5 * (two + jnp.where(near, roll(one, -layer), normal))
-            g[at] = jnp.concatenate([jnp.where(inside, first, one), g[at][32:]], axis=0)
-            g[4 + at] = jnp.concatenate([jnp.where(inside, last, two), g[4 + at][32:]], axis=0)
-        return g
-
-    def along_y(i, f):
-        g = nodal(f, 2, everything)
-        g = [g[s] * factor_ref[4 + s // 4 * 2 + s % 2] for s in range(8)]
-        for at in range(4):
-            here = at // 2 * 4 + at % 2
-            one, two = g[here], g[here + 2]
-            normal = normal_y_ref[i, at]
-            first = 0.5 * (one + jnp.where(lane_iy == 0, normal, roll(two, EZ)))
-            last = 0.5 * (two + jnp.where(lane_iy == EY - 1, normal, roll(one, -EZ)))
-            g[here] = jnp.where(b_edge, first, one)
-            g[here + 2] = jnp.where(b_edge, last, two)
-        return g
-
-    def along_z(f):
-        g = nodal(f, 3, everything)
-        g = [g[s] * factor_ref[8 + s // 2] for s in range(8)]
-        low = c_edge & (lane_iz > 0)
-        high = c_edge & (lane_iz < EZ - 1)
-        for at in range(4):
-            one, two = g[2 * at], g[2 * at + 1]
-            g[2 * at] = jnp.where(low, 0.5 * (one + roll(two, 1)), one)
-            g[2 * at + 1] = jnp.where(high, 0.5 * (two + roll(one, -1)), two)
-        return g
-
-    pairs = (
-        (lambda: along_y(1, 5), lambda: along_z(4)),
-        (lambda: along_z(3), lambda: along_x(1, 5)),
-        (lambda: along_x(0, 4), lambda: along_y(0, 3)),
-    )
-    uses = {0: ((1, 1), (2, 0)), 1: ((0, 0), (2, 1)), 2: ((0, 1), (1, 0))}
-    for i, (plus, minus) in enumerate(pairs):
-        one, two = plus(), minus()
-        folded = unfold([0.125 * (one[s] - two[s]) for s in range(8)])
-        for sector in range(8):
-            operand = folded[sector].astype(BF)
-            for axis, side in uses[i]:
-                vort_ref[axis, sector, :, side * count : (side + 1) * count] = operand
-
-    for axis in range(3):
-        flip = (4, 2, 1)[axis]
-        for sector in range(8):
-            source = vort_ref[axis, sector]
-            source = jnp.concatenate([source, source], axis=0)
-            which = 2 * axis + (1 if sector & flip else 0)
-            ws_ref[axis, sector ^ flip] = dot(second_ref[which], source)
+        if q == 1:
+            return [along_ref[pair, sector, at, lanes] for sector in range(8)]
+        if edge:
+            slot = (0, None, 1, 2)[q]
+            return [edge_ref[pair, slot, sector, at, lanes] for sector in range(8)]
+        return [gs_ref[pair, q, sector, at, lanes] for sector in range(8)]
+
+    chunk = 16
+
+    def vorticity(at, start, edge):
+        shape = (chunk, count)
+        lane_ix, lane_iy, lane_iz = positions(shape)
+        rows = lax.broadcasted_iota(jnp.int32, shape, 0) + start
+        on_a = rows < HO * HO
+        on_b = lax.rem(rows, HO * HO) < HO
+        on_c = lax.rem(rows, HO) == 0
+
+        def nodal(f, q, factor):
+            g = unfold(parts_of(f, q, at, edge))
+            return [g[s] * factor_ref[factor(s), at, :] for s in range(8)]
+
+        def along_x(i, f):
+            g = nodal(f, 1, lambda s: s % 4)
+            if edge:
+                for two in range(4):
+                    low, high = g[two], g[4 + two]
+                    normal = normal_x_ref[i, two, at, :]
+                    near = lane_ix == 0
+                    first = 0.5 * (low + jnp.where(near, normal, roll(high, layer)))
+                    last = 0.5 * (high + jnp.where(near, roll(low, -layer), normal))
+                    g[two] = jnp.where(on_a, first, low)
+                    g[4 + two] = jnp.where(on_a, last, high)
+            return g
+
+        def along_y(i, f):
+            g = nodal(f, 2, lambda s: 4 + s // 4 * 2 + s % 2)
+            for two in range(4):
+                here = two // 2 * 4 + two % 2
+                low, high = g[here], g[here + 2]
+                normal = normal_y_ref[i, two, at, :]
+                first = 0.5 * (low + jnp.where(lane_iy == 0, normal, roll(high, EZ)))
+                last = 0.5 * (high + jnp.where(lane_iy == EY - 1, normal, roll(low, -EZ)))
+                g[here] = jnp.where(on_b, first, low)
+                g[here + 2] = jnp.where(on_b, last, high)
+            return g
+
+        def along_z(f):
+            g = nodal(f, 3, lambda s: 8 + s // 2)
+            lower = on_c & (lane_iz > 0)
+            upper = on_c & (lane_iz < EZ - 1)
+            for two in range(4):
+                low, high = g[2 * two], g[2 * two + 1]
+                g[2 * two] = jnp.where(lower, 0.5 * (low + roll(high, 1)), low)
+                g[2 * two + 1] = jnp.where(upper, 0.5 * (high + roll(low, -1)), high)
+            return g
+
+        pairs = (
+            (lambda: along_y(1, 5), lambda: along_z(4)),
+            (lambda: along_z(3), lambda: along_x(1, 5)),
+            (lambda: along_x(0, 4), lambda: along_y(0, 3)),
+        )
+        for i, (plus, minus) in enumerate(pairs):
+            one, two = plus(), minus()
+            folded = unfold([0.125 * (one[s] - two[s]) for s in range(8)])
+            for sector in range(8):
+                vort_ref[i, sector, at, :] = folded[sector].astype(BF)
+
+    for step in range(2):
+        vorticity(slice(step * chunk, (step + 1) * chunk), step * chunk, True)
+
+    def vorticity_step(step, carry):
+        start = pl.multiple_of(step * chunk, chunk)
+        vorticity(pl.ds(start, chunk), start, False)
+        return carry
+
+    lax.fori_loop(2, ROWS // chunk, vorticity_step, 0)
 
     metric = [metric_ref[i : i + 1] for i in range(3)]
     inv = inv_ref[0]
     scaled = [inv * metric[i] for i in range(3)]
-
-    def body(step, total):
+    taken = ((1, 2), (2, 0), (0, 1))
+    terms = (((1, 0), (2, 1)), ((2, 0), (0, 1)), ((0, 0), (1, 1)))
+    for target in range(8):
+        slope = []
+        for axis in range(3):
+            flip = FLIPS[1 + axis]
+            sector = target ^ flip
+            source = jnp.concatenate([vort_ref[i, sector] for i in taken[axis]], axis=1)
+            source = jnp.concatenate([source, source], axis=0)
+            at = second_at + (2 * axis + (1 if sector & flip else 0)) * ROWS
+            slope.append(dot(const_ref[at : at + ROWS, :], source))
+        for i in range(3):
+            (one, half), (two, other) = terms[i]
+            plus = scaled[one] * slope[one][:, half * count : (half + 1) * count]
+            minus = scaled[two] * slope[two][:, other * count : (other + 1) * count]
+            if i == 0:
+                linear_ref[i, target] = along_ref[3, target, :, 0:count] * metric[0] + (plus - minus)
+            else:
+                near = edge_ref[3, i, target, :, 0:count] * metric[i]
+                far = gs_ref[3, 1 + i, target, 32:, 0:count] * metric[i]
+                linear_ref[i, target, 0:32, :] = near + (plus - minus)[0:32]
+                linear_ref[i, target, 32:, :] = far + (plus - minus)[32:]
+
+    def body(edge, step, total):
         at = pl.ds(pl.multiple_of(step * 8, 8), 8)
         for side in range(2):
-            total = total + quad_ref[at, :] * energy_of(at, side)
+            total = total + quad_ref[at, :] * energy_of(at, side, edge)
         return total
 
-    def energy_of(at, side):
+    def energy_of(at, side, edge):
         def unfold_half(parts):
             return unfold4([signed(parts[s], parts[4 + s], side) for s in range(4)])
 
         def part(f, q):
-            pair, half = PLACE[f]
-            lanes = slice(half * count, (half + 1) * count)
-            return unfold_half([gs_ref[pair, q, s, at, lanes] for s in range(8)])
-
-        def curl(axis, half, sector):
-            return ws_ref[axis, sector, at, half * count : (half + 1) * count]
+            return unfold_half(parts_of(f, q, at, edge))
 
         base = [[item * metric[j] for item in part(j, 0)] for j in range(3)]
         dual = [part(3 + j, 0) for j in range(3)]
         energy = spread = None
-        terms = (((1, 0), (2, 1)), ((2, 0), (0, 1)), ((0, 0), (1, 1)))
         for i in range(3):
-            plus, minus = terms[i]
-            linear = []
-            for s in range(8):
-                viscous = scaled[plus[0]] * curl(plus[0], plus[1], s)
-                viscous = viscous - scaled[minus[0]] * curl(minus[0], minus[1], s)
-                linear.append(gs_ref[1, 1 + i, s, at, count : 2 * count] * metric[i] + viscous)
-            total = unfold_half(linear)
+            total = unfold_half([linear_ref[i, s, at, :] for s in range(8)])
             for j in range(3):
                 slope = part(3 + i, 1 + j)
                 total = [total[s] - base[j][s] * slope[s] for s in range(4)]
@@ -634,14 +742,16 @@
         energy = [energy[s] + spread[s] * spread[s] for s in range(4)]
         return (energy[0] + energy[1]) + (energy[2] + energy[3])
 
-    total = lax.fori_loop(0, ROWS // 8, body, jnp.zeros((8, count), F32))
+    total = jnp.zeros((8, count), F32)
+    total = lax.fori_loop(0, 4, functools.partial(body, True), total)
+    total = lax.fori_loop(4, ROWS // 8, functools.partial(body, False), total)
     weighted = jnp.sum(total, axis=0, keepdims=True)
     result = jnp.sqrt(weighted / 8.0) / float(ORDER_OUT**2)
     high, mid, low = split3(result)
     stacked = jnp.concatenate(
         [high.astype(F32), mid.astype(F32), low.astype(F32), jnp.zeros((13, count), F32)], axis=0
     )
-    moved = dot(stacked.astype(BF), slot_matrix(emap_ref, count))
+    moved = dot(stacked.astype(BF), slots_ref[...])
     out_ref[...] = moved[0:1] + moved[1:2] + moved[2:3]
 
 
@@ -657,31 +767,45 @@
     return plus + minus
 
 
-LIMIT = 60 * 1024 * 1024
+MIB = 1024 * 1024
 
 
 def per_device(fields, elem_map, metric, inv_reynolds):
-    refine, second, lift_x, lift_y, quad, (line, ends_value) = tables()
+    const, weights, (line, ends_value) = tables()
     count = fields.shape[-1]
     vmem = pl.BlockSpec(memory_space=pltpu.VMEM)
     smem = pl.BlockSpec(memory_space=pltpu.SMEM)
-    params = pltpu.CompilerParams(vmem_limit_bytes=LIMIT)
+
+    def params(mib):
+        return pltpu.CompilerParams(vmem_limit_bytes=mib * MIB)
 
     def struct(shape, dtype=F32):
         return jax.ShapeDtypeStruct(shape, dtype)
 
-    coarse, local_metric, message = pl.pallas_call(
+    small = jnp.concatenate([elem_map.astype(F32), metric], axis=0)
+    slots, local_metric, message = pl.pallas_call(
         functools.partial(first_kernel, line),
         out_shape=(
-            struct((7, NI, NI, NI, count)),
+            struct((count, count), BF),
             struct((8, count)),
             struct((9 * 64 + 16, count), BF),
         ),
-        in_specs=[vmem] * 3,
+        in_specs=[vmem] * 2,
         out_specs=(vmem,) * 3,
-        compiler_params=params,
+        compiler_params=params(6),
         name="first",
-    )(fields, elem_map, metric)
+    )(fields, small)
+    coarse = pl.pallas_call(
+        own_kernel,
+        out_shape=struct((7, NI, NI, NI, count)),
+        in_specs=[vmem] * 2,
+        out_specs=vmem,
+        compiler_params=params(6),
+        cost_estimate=pl.CostEstimate(
+            flops=2 * fields.size * count, bytes_accessed=3 * 10**6, transcendentals=0
+        ),
+        name="own",
+    )(fields, slots)
 
     azim = lax.axis_size("azim")
     if azim == 2:
@@ -708,7 +832,7 @@
         ),
         in_specs=[smem] + [vmem] * 3,
         out_specs=(vmem,) * 5,
-        compiler_params=params,
+        compiler_params=params(12),
         name="second",
     )(parity, coarse, local_metric, halo)
 
@@ -723,38 +847,54 @@
         got_b = lax.ppermute(to_a, "strm", [(i, (i + 1) % streams) for i in range(streams)])
         got_a = lax.ppermute(to_b, "strm", [((i + 1) % streams, i) for i in range(streams)])
 
-    result = pl.pallas_call(
-        functools.partial(third_kernel, ends_value),
-        out_shape=struct((1, count)),
-        in_specs=[smem] * 2 + [vmem] * 12,
+    table_of = jnp.asarray(const)
+    raw = pl.pallas_call(
+        third_kernel,
+        out_shape=struct((PAIRS, 4, 8, ROWS, 2 * count)),
+        in_specs=[vmem] * 2,
         out_specs=vmem,
         scratch_shapes=[
-            pltpu.VMEM((8, HO * HO * NI, count), F32),
-            pltpu.VMEM((4, 8, ROWS, 2 * count), BF),
-            pltpu.VMEM((4, 4, 8, ROWS, 2 * count), F32),
-            pltpu.VMEM((3, 8, ROWS, 2 * count), BF),
-            pltpu.VMEM((3, 8, ROWS, 2 * count), F32),
+            pltpu.VMEM((8, HO * HI * NI, count), F32),
+            pltpu.VMEM((PAIRS, 8, ROWS, 2 * count), BF),
+        ],
+        compiler_params=params(6),
+        cost_estimate=pl.CostEstimate(
+            flops=4 * 10**9, bytes_accessed=20 * 10**6, transcendentals=0
+        ),
+        name="third",
+    )(extended, table_of)
+
+    result = pl.pallas_call(
+        functools.partial(fourth_kernel, ends_value, weights),
+        out_shape=struct((1, count)),
+        in_specs=[smem] * 2 + [vmem] * 9,
+        out_specs=vmem,
+        scratch_shapes=[
+            pltpu.VMEM((8, NI * NI, count), F32),
+            pltpu.VMEM((PAIRS, 8, ROWS, 2 * count), F32),
+            pltpu.VMEM((PAIRS, 3, 8, 32, 2 * count), F32),
+            pltpu.VMEM((3, 8, ROWS, count), BF),
+            pltpu.VMEM((3, 8, ROWS, count), F32),
             pltpu.VMEM((12, ROWS, count), F32),
             pltpu.VMEM((2, 4, 32, count), F32),
             pltpu.VMEM((2, 4, ROWS, count), F32),
+            pltpu.VMEM((ROWS, count), F32),
+            pltpu.VMEM((PAIRS, 8, 48, 2 * count), BF),
         ],
-        compiler_params=params,
-        name="third",
+        compiler_params=params(20),
+        name="fourth",
     )(
         parity,
         inv_reynolds,
+        raw,
         extended,
         ends,
         table,
         local_metric,
-        elem_map,
+        slots,
         got_a,
         got_b,
-        jnp.asarray(refine),
-        jnp.asarray(second),
-        jnp.asarray(lift_x),
-        jnp.asarray(lift_y),
-        jnp.asarray(quad),
+        table_of,
     )
     return result.reshape(count)
 

time: 33.6 us -> 25.7 us (0.76)
  Pallas kernels: 20 us -> 14.2 us
  waiting for transfers between devices: 4.57 us -> 0.01 us
  other arithmetic: 0 us -> 1.66 us
  local copies, waits for them, and re-layouts: 1.3 us -> 2.36 us
    pallas_call x1, Pallas kernels: 3.53 us -> 0.6 us  [per_device(): pl.pallas_call(functools.partial(second_kernel, line), out_shape=(struct(...]
    ppermute x1, waiting for transfers between devices: 2.6 us -> 0.01 us  [per_device(): got_b = lax.ppermute(to_b, 'strm', far)]
    pallas_call x1, Pallas kernels: 2.89 us -> 1.13 us  [per_device(): pl.pallas_call(functools.partial(first_kernel, line), out_shape=(struct((...]
    ppermute x1, waiting for transfers between devices: 1.22 us -> 0.01 us  [per_device(): halo = lax.ppermute(message, 'azim', [(0, 1), (1, 0)])]
    pallas_call x1 -> x3, Pallas kernels: 13.6 us -> 12.5 us  [the longest x1 7.68 us: per_device(): pl.pallas_call(functools.partial(fourth_kernel, ends_value, weights), out...]
    unnamed x6, local copies, waits for them, and re-layouts: 1.3 us -> 2.36 us
    concatenate x0 -> x1, other arithmetic: none -> 0.85 us  [per_device(): small = jnp.concatenate([elem_map.astype(F32), metric], axis=0)]
    convert_element_type x0 -> x1, other arithmetic: none -> 0.81 us  [per_device(): small = jnp.concatenate([elem_map.astype(F32), metric], axis=0)]
  transfers between devices with their start and end apart: 3 -> 3, of which waited for: 3 -> 0; matrix products, arithmetic and copies ran while one was open for 0% -> 0% of each run, Pallas kernels for 0% -> 19%
where the time goes in v1:
time: 25.7 us; the launch traced here: 25.6 us
  Pallas kernels  14.2 us (55%)
  starting transfers between devices  6.61 us (26%)
  local copies, waits for them, and re-layouts  2.36 us (9%)
  other arithmetic  1.66 us (6%)
  between operations  0.71 us (3%)
    pallas_call x1, Pallas kernels, per_device(): pl.pallas_call(functools.partial(fourth_kernel, ends_value, weights), out...  7.68 us
    pallas_call x1, Pallas kernels, per_device(): pl.pallas_call(third_kernel, out_shape=struct((PAIRS, 4, 8, ROWS, 2 * cou...  4.42 us
    ppermute x1, starting transfers between devices, per_device(): got_b = lax.ppermute(to_b, 'strm', far)  3.57 us
    ppermute x1, starting transfers between devices, per_device(): got_a = lax.ppermute(to_a, 'strm', near)  2.55 us
    unnamed x6, local copies, waits for them, and re-layouts  2.36 us
    pallas_call x1, Pallas kernels, per_device(): pl.pallas_call(functools.partial(first_kernel, line), out_shape=(struct((...  1.13 us
    concatenate x1, other arithmetic, per_device(): small = jnp.concatenate([elem_map.astype(F32), metric], axis=0)  0.85 us
    convert_element_type x1, other arithmetic, per_device(): small = jnp.concatenate([elem_map.astype(F32), metric], axis=0)  0.81 us
  transfers between devices with their start and end apart: 3, of which 0 were waited for; matrix products, arithmetic and copies ran while one was open for 0% of the time, Pallas kernels for 19%

profile of v1, /device:TPU:0, one launch (start us, length us, event | category | flops | bytes accessed | tf_op | source)
XLA Modules:
  0.0 25.6 jit_solution(15386826243254266889)
XLA Ops:
  0.0 0.0 copy-start
  0.0 0.8 %convert_element_type.3 = f32[1,128]{1,0:T(1,128)S(1)} convert(s32[1,128]{1,0:T(1,128)} %param.6) | non-fusion elementwise | flops 128 | bytes 1024 | tf_op jit(solution)/shard_map/convert_element_type | solution.py:785
  0.8 0.9 %pad_maximum_fusion.small_ref = f32[4,128]{1,0:T(4,128)S(1)} fusion(f32[3,128]{1,0:T(4,128)} %param.7, f32[1,128]{1,0:T(1,128)S(1)} %convert_element_type.3), kind=kLoop, calls=%fused_computation | loop fusion | flops 512 | bytes 4096 | tf_op jit(solution)/shard_map/concatenate | solution.py:785
  1.7 0.0 copy-start.1
  1.7 1.2 %copy-done.1 = bf16[7,512,128]{2,1,0:T(8,128)(2,1)S(1)} copy-done((bf16[7,512,128]{2,1,0:T(8,128)(2,1)S(1)}, bf16[7,512,128]{2,1,0:T(8,128)(2,1)}, u32[]{:S(2)}) %copy-start.1) | copy-done | bytes 917528
  2.8 1.1 %first.1 = (bf16[128,128]{1,0:T(8,128)(2,1)S(1)}, f32[8,128]{1,0:T(8,128)S(1)}, bf16[592,128]{1,0:T(8,128)(2,1)}) custom-call(bf16[7,512,128]{2,1,0:T(8,128)(2,1)S(1)} %copy-done.1, f32[4,128]{1,0:T(4,128)S(1)} %pad_maximum_fusion.small_ref), custom_call_target="tpu_custom_call" | custom-call | tf_op jit(solution)/shard_map/first/pallas_call | solution.py:786
  4.0 0.5 %collective-permute-start = (bf16[592,128]{1,0:T(8,128)(2,1)}, bf16[592,128]{1,0:T(8,128)(2,1)S(1)}, u32[]{:S(2)}, u32[]{:S(2)}) collective-permute-start(bf16[592,128]{1,0:T(8,128)(2,1)} %get-tuple-element.15), channel_id=1, source_target_pairs={{0,1},{1,0},{2,3},{3,2},{4,5},{5,4},{6,7},{7,6},{8,9},{9,8},{10,11... | collective-permute-start | bytes 454664 | tf_op jit(solution)/shard_map/ppermute | solution.py:812
  5.1 0.0 copy-start.2
  5.1 1.2 %copy-done.2 = bf16[7,512,128]{2,1,0:T(8,128)(2,1)S(1)} copy-done((bf16[7,512,128]{2,1,0:T(8,128)(2,1)S(1)}, bf16[7,512,128]{2,1,0:T(8,128)(2,1)}, u32[]{:S(2)}) %copy-start.2) | copy-done | bytes 917528
  6.3 0.4 %own.1.coarse_ref = f32[7,8,8,8,128]{4,3,2,1,0:T(8,128)S(1)} custom-call(bf16[7,512,128]{2,1,0:T(8,128)(2,1)S(1)} %copy-done.2, bf16[128,128]{1,0:T(8,128)(2,1)S(1)} %get-tuple-element.13.slots_ref), custom_call_target="tpu_custom_call" | custom-call | flops 117440512 | bytes 3000000 | tf_op jit(solution)/shard_map/own/pallas_call | solution.py:798
  6.7 0.0 collective-permute-done.halo_ref
  6.7 0.6 %second.1 = (f32[7,8,10,8,128]{4,3,2,1,0:T(8,128)S(1)}, f32[2,8,8,128]{3,2,1,0:T(8,128)S(1)}, f32[24,128]{1,0:T(8,128)S(1)}, bf16[400,128]{1,0:T(8,128)(2,1)S(1)}, bf16[400,128]{1,0:T(8,128)(2,1)S(1)}) custom-call(s32[1]{0:T(128)} %bitcast.par_ref, f32[7,8,8,8,128]{4,3,2,1,0:T(8,128)S(1)} %own.1.coarse_ref, f32[8,128]{1,0:T(8,128)S(1)} %get-tuple-element.14.metric_ref, ...), custom_call_target="tpu_custom_call" | custom-call | tf_op jit(solution)/shard_map/second/pallas_call | solution.py:824
  7.3 2.6 %collective-permute-start.1 = (bf16[400,128]{1,0:T(8,128)(2,1)S(1)}, bf16[400,128]{1,0:T(8,128)(2,1)S(1)}, u32[]{:S(2)}, u32[]{:S(2)}) collective-permute-start(bf16[400,128]{1,0:T(8,128)(2,1)S(1)} %get-tuple-element.19), channel_id=1, source_target_pairs={{0,2},{2,0},{4,6},{6,4},{8,10},{10,8},{12,14},{14,12},{1,3},{3,1},... | collective-permute-start | bytes 307208 | tf_op jit(solution)/shard_map/ppermute | solution.py:844
  9.9 3.6 %collective-permute-start.2 = (bf16[400,128]{1,0:T(8,128)(2,1)S(1)}, bf16[400,128]{1,0:T(8,128)(2,1)S(1)}, u32[]{:S(2)}, u32[]{:S(2)}) collective-permute-start(bf16[400,128]{1,0:T(8,128)(2,1)S(1)} %get-tuple-element.20), channel_id=1, source_target_pairs={{2,4},{4,2},{6,8},{8,6},{10,12},{12,10},{14,0},{0,14},{3,5},{5,3},... | collective-permute-start | bytes 307208 | tf_op jit(solution)/shard_map/ppermute | solution.py:845
  13.4 0.0 copy-done
  13.4 4.4 %third.1.gs_ref = f32[4,4,8,128,256]{4,3,2,1,0:T(8,128)S(1)} custom-call(f32[7,8,10,8,128]{4,3,2,1,0:T(8,128)S(1)} %get-tuple-element.16.ext_ref, bf16[6400,256]{1,0:T(8,128)(2,1)S(1)} %copy-done), custom_call_target="tpu_custom_call" | custom-call | flops 4000000000 | bytes 20000000 | tf_op jit(solution)/shard_map/third/pallas_call | solution.py:851
  17.9 0.0 collective-permute-done.1.ra_ref
  17.9 0.0 collective-permute-done.2.rb_ref
  17.9 7.7 %fourth.1 = f32[1,128]{1,0:T(1,128)} custom-call(s32[1]{0:T(128)} %bitcast.par_ref, f32[1]{0:T(128)S(6)} %copy.6.inv_ref, f32[4,4,8,128,256]{4,3,2,1,0:T(8,128)S(1)} %third.1.gs_ref, f32[7,8,10,8,128]{4,3,2,1,0:T(8,128)S(1)} %get-tuple-element.16.ext_ref, f32[2,8,8,128]{3,2,1,0:T(8,128)S(1)} %get-tuple-element.17.ends_ref, ...), custom_call_target="tpu_custom_call" | custom-call | tf_op jit(solution)/shard_map/fourth/pallas_call | solution.py:867
Async XLA Ops:
  0.0 13.4 %copy-start = (bf16[6400,256]{1,0:T(8,128)(2,1)S(1)}, bf16[6400,256]{1,0:T(8,128)(2,1)}, u32[]{:S(2)}) copy-start(bf16[6400,256]{1,0:T(8,128)(2,1)} %constant.13.clone.const_ref) | copy-start | bytes 9830404
  1.7 1.2 %copy-start.1 = (bf16[7,512,128]{2,1,0:T(8,128)(2,1)S(1)}, bf16[7,512,128]{2,1,0:T(8,128)(2,1)}, u32[]{:S(2)}) copy-start(bf16[7,512,128]{2,1,0:T(8,128)(2,1)} %fields_ref.1) | copy-start | bytes 2752516
  4.0 2.7 %collective-permute-start = (bf16[592,128]{1,0:T(8,128)(2,1)}, bf16[592,128]{1,0:T(8,128)(2,1)S(1)}, u32[]{:S(2)}, u32[]{:S(2)}) collective-permute-start(bf16[592,128]{1,0:T(8,128)(2,1)} %get-tuple-element.15), channel_id=1, source_target_pairs={{0,1},{1,0},{2,3},{3,2},{4,5},{5,4},{6,7},{7,6},{8,9},{9,8},{10,11... | collective-permute-start | bytes 454664 | tf_op jit(solution)/shard_map/ppermute | solution.py:812
  5.1 1.2 %copy-start.2 = (bf16[7,512,128]{2,1,0:T(8,128)(2,1)S(1)}, bf16[7,512,128]{2,1,0:T(8,128)(2,1)}, u32[]{:S(2)}) copy-start(bf16[7,512,128]{2,1,0:T(8,128)(2,1)} %fields_ref.1) | copy-start | bytes 2752516
  7.3 10.6 %collective-permute-start.1 = (bf16[400,128]{1,0:T(8,128)(2,1)S(1)}, bf16[400,128]{1,0:T(8,128)(2,1)S(1)}, u32[]{:S(2)}, u32[]{:S(2)}) collective-permute-start(bf16[400,128]{1,0:T(8,128)(2,1)S(1)} %get-tuple-element.19), channel_id=1, source_target_pairs={{0,2},{2,0},{4,6},{6,4},{8,10},{10,8},{12,14},{14,12},{1,3},{3,1},... | collective-permute-start | bytes 307208 | tf_op jit(solution)/shard_map/ppermute | solution.py:844
  9.9 8.0 %collective-permute-start.2 = (bf16[400,128]{1,0:T(8,128)(2,1)S(1)}, bf16[400,128]{1,0:T(8,128)(2,1)S(1)}, u32[]{:S(2)}, u32[]{:S(2)}) collective-permute-start(bf16[400,128]{1,0:T(8,128)(2,1)S(1)} %get-tuple-element.20), channel_id=1, source_target_pairs={{2,4},{4,2},{6,8},{8,6},{10,12},{12,10},{14,0},{0,14},{3,5},{5,3},... | collective-permute-start | bytes 307208 | tf_op jit(solution)/shard_map/ppermute | solution.py:845

commit v2 on v1

--- a/solution.py
+++ b/solution.py
@@ -162,10 +162,9 @@
         matrix = np.concatenate(parts)
         return np.pad(matrix, ((0, 0), (0, 2 * ROWS - matrix.shape[1]))).astype(jnp.bfloat16)
 
+    refine = refine.reshape(-1, 2 * ROWS)
     const = np.concatenate(
-        [refine.reshape(-1, 2 * ROWS)]
-        + seams
-        + [second.reshape(-1, 2 * ROWS), one_term(lift_x), one_term(lift_y)]
+        seams + [second.reshape(-1, 2 * ROWS), one_term(lift_x), one_term(lift_y)]
     )
     half_weights = [float(v) for v in weights[:HO]]
     line = []
@@ -174,12 +173,16 @@
         weights_in[[0, NO - 1]] = 0.0
         line.append(([float(v) for v in weights_in @ interp], float(slopes[end, far])))
     ends = (float(slopes[0, 0]), float(slopes[NO - 1, NO - 1]))
-    return const, half_weights, (line, ends)
+    return refine, const, half_weights, (line, ends)
 
 
 def dot(a, b, contract_last=False):
     dims = (((1,), (1 if contract_last else 0,)), ((), ()))
     return lax.dot_general(a, b, dims, preferred_element_type=F32)
+
+
+def is_even(even_ring):
+    return lax.rem(lax.axis_index("strm"), 2) == 0 if even_ring else True
 
 
 def rows3(x):
@@ -237,12 +240,48 @@
     return one, two
 
 
-def first_kernel(line, fields, small_ref, slots_ref, metric_out, msg_ref):
+def chunks(source, target, sem, count=8):
+    step = source.shape[0] // count
+    return [
+        pltpu.make_async_copy(
+            source.at[i * step : (i + 1) * step], target.at[i * step : (i + 1) * step], sem.at[i]
+        )
+        for i in range(count)
+    ]
+
+
+def first_kernel(
+    line,
+    fields_hbm,
+    emap_hbm,
+    metric_hbm,
+    table_hbm,
+    slots_ref,
+    metric_out,
+    msg_ref,
+    coarse_ref,
+    table_ref,
+    fields,
+    emap,
+    metric,
+    sem,
+):
     count = fields.shape[-1]
-    local = lax.broadcasted_iota(jnp.int32, (count, count), 0).astype(F32)
-    slots = (local == small_ref[0:1]).astype(F32).astype(BF)
+    order = (3, 5, 4, 0, 1, 2, 6)
+    small = [
+        pltpu.make_async_copy(emap_hbm, emap, sem.at[7]),
+        pltpu.make_async_copy(metric_hbm, metric, sem.at[8]),
+    ]
+    large = [pltpu.make_async_copy(fields_hbm.at[f], fields.at[f], sem.at[f]) for f in order]
+    tables_copies = chunks(table_hbm, table_ref, sem.at[pl.ds(9, 8)])
+    for copy in small + large + tables_copies:
+        copy.start()
+    for copy in small:
+        copy.wait()
+    local = lax.broadcasted_iota(jnp.int32, (count, count), 0)
+    slots = (local == emap[...]).astype(F32).astype(BF)
     slots_ref[...] = slots
-    high, mid, low = split3(small_ref[1:4])
+    high, mid, low = split3(metric[...])
     pad = jnp.zeros((7, count), F32)
     stacked = jnp.concatenate([high.astype(F32), mid.astype(F32), low.astype(F32), pad], axis=0)
     moved = dot(stacked.astype(BF), slots, True)
@@ -252,21 +291,18 @@
     tail = jnp.concatenate([high, local - high, jnp.zeros((10, count), F32)], axis=0)
     msg_ref[9 * 64 : 9 * 64 + 16, :] = tail.astype(BF)
     iy = positions((1, 1, count))[1]
-    for f in range(7):
+    for f, copy in zip(order, large):
+        copy.wait()
         values = dot(fields[f], slots, True).reshape(NI, NI, NI, count)
+        coarse_ref[f] = values
         face = jnp.where(iy == 0, values[:, 0], values[:, NI - 1])
         msg_ref[f * 64 : f * 64 + 64, :] = rows2(face).astype(BF)
         if f in (3, 5):
             low, high = end_lines(line, [values[:, b] for b in range(NI)], EZ)
             at = (7 + (f == 5)) * 64
             msg_ref[at : at + 64, :] = rows2(jnp.where(iy == 0, low, high)).astype(BF)
-
-
-def own_kernel(fields_ref, slots_ref, coarse_ref):
-    count = fields_ref.shape[-1]
-    for f in range(7):
-        values = dot(fields_ref[f], slots_ref[...], True)
-        coarse_ref[f] = values.reshape(NI, NI, NI, count)
+    for copy in tables_copies:
+        copy.wait()
 
 
 def from_azim(x, iy):
@@ -287,7 +323,7 @@
 
 
 def second_kernel(
-    line, par_ref, coarse_ref, metric_ref, halo_ref, ext_ref, ends_ref, table_ref, a_ref, b_ref
+    line, even_ring, coarse_ref, metric_ref, halo_ref, ext_ref, ends_ref, table_ref, a_ref, b_ref
 ):
     count = coarse_ref.shape[-1]
     layer = EY * EZ
@@ -331,7 +367,7 @@
     blocks.append(jnp.concatenate(extra + [high, table - high, spare], axis=0))
 
     ix = positions((SEAM, count))[0]
-    even = par_ref[0] == 0
+    even = is_even(even_ring)
     half = len(blocks) // 2
     for i in range(half):
         one, two = blocks[i], blocks[half + i]
@@ -364,11 +400,15 @@
     ]
 
 
-def third_kernel(ext_ref, const_ref, gs_ref, tmp_ref, xs_ref):
+def third_kernel(ext_ref, const_ref, later_hbm, gs_ref, later_ref, tmp_ref, xs_ref, sem):
     count = ext_ref.shape[-1]
     width = HO * HI
     iz = positions((width, count))[2]
     zeros = jnp.zeros((HI, count), F32)
+
+    copies = chunks(later_hbm, later_ref, sem)
+    for copy in copies:
+        copy.start()
     for f in range(7):
         pair, side = PLACE[f]
         lanes = slice(side * count, (side + 1) * count)
@@ -401,12 +441,14 @@
         return carry
 
     lax.fori_loop(0, 8, refine, 0)
+    for copy in copies:
+        copy.wait()
 
 
 def fourth_kernel(
     ends_value,
     weights,
-    par_ref,
+    even_ring,
     inv_ref,
     gs_ref,
     ext_ref,
@@ -431,10 +473,10 @@
 ):
     count = ext_ref.shape[-1]
     layer = EY * EZ
-    even = par_ref[0] == 0
+    even = is_even(even_ring)
     ix = positions((SEAM, count))[0]
     end_low, end_high = ends_value
-    seam_at = 8 * 4 * ROWS
+    seam_at = 0
     second_at = seam_at + 4 * SEAM_ROWS
     lift_x_at = second_at + 6 * ROWS
     lift_y_at = lift_x_at + ROWS
@@ -771,10 +813,9 @@
 
 
 def per_device(fields, elem_map, metric, inv_reynolds):
-    const, weights, (line, ends_value) = tables()
+    refine, const, weights, (line, ends_value) = tables()
     count = fields.shape[-1]
     vmem = pl.BlockSpec(memory_space=pltpu.VMEM)
-    smem = pl.BlockSpec(memory_space=pltpu.SMEM)
 
     def params(mib):
         return pltpu.CompilerParams(vmem_limit_bytes=mib * MIB)
@@ -782,30 +823,31 @@
     def struct(shape, dtype=F32):
         return jax.ShapeDtypeStruct(shape, dtype)
 
-    small = jnp.concatenate([elem_map.astype(F32), metric], axis=0)
-    slots, local_metric, message = pl.pallas_call(
+    hbm = pl.BlockSpec(memory_space=pltpu.HBM)
+    inputs = [
+        pltpu.with_memory_space_constraint(item, pltpu.HBM)
+        for item in (fields, elem_map, metric, jnp.asarray(refine), jnp.asarray(const))
+    ]
+    slots, local_metric, message, coarse, refine = pl.pallas_call(
         functools.partial(first_kernel, line),
         out_shape=(
             struct((count, count), BF),
             struct((8, count)),
             struct((9 * 64 + 16, count), BF),
+            struct((7, NI, NI, NI, count)),
+            struct(refine.shape, BF),
         ),
-        in_specs=[vmem] * 2,
-        out_specs=(vmem,) * 3,
+        in_specs=[hbm] * 4,
+        out_specs=(vmem,) * 5,
+        scratch_shapes=[
+            pltpu.VMEM(fields.shape, BF),
+            pltpu.VMEM(elem_map.shape, jnp.int32),
+            pltpu.VMEM(metric.shape, F32),
+            pltpu.SemaphoreType.DMA((17,)),
+        ],
         compiler_params=params(6),
         name="first",
-    )(fields, small)
-    coarse = pl.pallas_call(
-        own_kernel,
-        out_shape=struct((7, NI, NI, NI, count)),
-        in_specs=[vmem] * 2,
-        out_specs=vmem,
-        compiler_params=params(6),
-        cost_estimate=pl.CostEstimate(
-            flops=2 * fields.size * count, bytes_accessed=3 * 10**6, transcendentals=0
-        ),
-        name="own",
-    )(fields, slots)
+    )(*inputs[:4])
 
     azim = lax.axis_size("azim")
     if azim == 2:
@@ -816,13 +858,10 @@
         iy = (jnp.arange(count) // EZ) % EY
         halo = jnp.where(iy >= EY // 2, ahead, behind)
 
-    place = lax.axis_index("strm")
     streams = lax.axis_size("strm")
-    parity = lax.rem(place, 2).astype(jnp.int32).reshape(1)
-    if streams % 2:
-        parity = jnp.zeros((1,), jnp.int32)
+    even_ring = streams % 2 == 0
     extended, ends, table, to_a, to_b = pl.pallas_call(
-        functools.partial(second_kernel, line),
+        functools.partial(second_kernel, line, even_ring),
         out_shape=(
             struct((7, NI, EXT, NI, count)),
             struct((2, NI, NI, count)),
@@ -830,13 +869,13 @@
             struct((5 * SEAM, count), BF),
             struct((5 * SEAM, count), BF),
         ),
-        in_specs=[smem] + [vmem] * 3,
+        in_specs=[vmem] * 3,
         out_specs=(vmem,) * 5,
         compiler_params=params(12),
         name="second",
-    )(parity, coarse, local_metric, halo)
-
-    if streams % 2 == 0:
+    )(coarse, local_metric, halo)
+
+    if even_ring:
         near = [(i, i ^ 1) for i in range(streams)]
         far = []
         for i in range(1, streams, 2):
@@ -847,27 +886,27 @@
         got_b = lax.ppermute(to_a, "strm", [(i, (i + 1) % streams) for i in range(streams)])
         got_a = lax.ppermute(to_b, "strm", [((i + 1) % streams, i) for i in range(streams)])
 
-    table_of = jnp.asarray(const)
-    raw = pl.pallas_call(
+    raw, const = pl.pallas_call(
         third_kernel,
-        out_shape=struct((PAIRS, 4, 8, ROWS, 2 * count)),
-        in_specs=[vmem] * 2,
-        out_specs=vmem,
+        out_shape=(struct((PAIRS, 4, 8, ROWS, 2 * count)), struct(const.shape, BF)),
+        in_specs=[vmem, vmem, hbm],
+        out_specs=(vmem, vmem),
         scratch_shapes=[
             pltpu.VMEM((8, HO * HI * NI, count), F32),
             pltpu.VMEM((PAIRS, 8, ROWS, 2 * count), BF),
+            pltpu.SemaphoreType.DMA((8,)),
         ],
-        compiler_params=params(6),
+        compiler_params=params(8),
         cost_estimate=pl.CostEstimate(
             flops=4 * 10**9, bytes_accessed=20 * 10**6, transcendentals=0
         ),
         name="third",
-    )(extended, table_of)
+    )(extended, refine, inputs[4])
 
     result = pl.pallas_call(
-        functools.partial(fourth_kernel, ends_value, weights),
+        functools.partial(fourth_kernel, ends_value, weights, even_ring),
         out_shape=struct((1, count)),
-        in_specs=[smem] * 2 + [vmem] * 9,
+        in_specs=[pl.BlockSpec(memory_space=pltpu.SMEM)] + [vmem] * 9,
         out_specs=vmem,
         scratch_shapes=[
             pltpu.VMEM((8, NI * NI, count), F32),
@@ -884,7 +923,6 @@
         compiler_params=params(20),
         name="fourth",
     )(
-        parity,
         inv_reynolds,
         raw,
         extended,
@@ -894,7 +932,7 @@
         slots,
         got_a,
         got_b,
-        table_of,
+        const,
     )
     return result.reshape(count)
 

time: 25.7 us -> 23.8 us (0.926)
  local copies, waits for them, and re-layouts: 2.36 us -> 0 us
  other arithmetic: 1.66 us -> 0 us
  Pallas kernels: 14.2 us -> 15.5 us
  starting transfers between devices: 6.61 us -> 7.04 us
  waiting for transfers between devices: 0.01 us -> 0.37 us
    unnamed x6 -> x0, local copies, waits for them, and re-layouts: 2.36 us -> none
    pallas_call x1, Pallas kernels: 1.13 us -> 2.76 us  [per_device(): pl.pallas_call(functools.partial(first_kernel, line), out_shape=(struct((...]
    concatenate x1 -> x0, other arithmetic: 0.85 us -> none  [per_device(): small = jnp.concatenate([elem_map.astype(F32), metric], axis=0)]
    convert_element_type x1 -> x0, other arithmetic: 0.81 us -> none  [per_device(): small = jnp.concatenate([elem_map.astype(F32), metric], axis=0)]
    ppermute x1, waiting for transfers between devices: 0.01 us -> 0.36 us  [per_device(): halo = lax.ppermute(message, 'azim', [(0, 1), (1, 0)])]
    ppermute x1, starting transfers between devices: 2.55 us -> 2.9 us  [per_device(): got_a = lax.ppermute(to_a, 'strm', near)]
    pallas_call x4 -> x3, Pallas kernels: 13.1 us -> 12.8 us  [the longest x1 7.67 us: per_device(): pl.pallas_call(functools.partial(fourth_kernel, ends_value, weights, even...]
  transfers between devices with their start and end apart: 3 -> 3, of which waited for: 0 -> 1; matrix products, arithmetic and copies ran while one was open for 0% -> 0% of each run, Pallas kernels for 19% -> 19%
where the time goes in v2:
time: 23.8 us; the launch traced here: 23.6 us
  Pallas kernels  15.5 us (65%)
  starting transfers between devices  7.04 us (30%)
  between operations  0.69 us (3%)
  waiting for transfers between devices  0.37 us (2%)
    pallas_call x1, Pallas kernels, per_device(): pl.pallas_call(functools.partial(fourth_kernel, ends_value, weights, even...  7.67 us
    pallas_call x1, Pallas kernels, per_device(): pl.pallas_call(third_kernel, out_shape=(struct((PAIRS, 4, 8, ROWS, 2 * co...  4.5 us
    ppermute x1, starting transfers between devices, per_device(): got_b = lax.ppermute(to_b, 'strm', far)  3.58 us
    ppermute x1, starting transfers between devices, per_device(): got_a = lax.ppermute(to_a, 'strm', near)  2.9 us
    pallas_call x1, Pallas kernels, per_device(): pl.pallas_call(functools.partial(first_kernel, line), out_shape=(struct((...  2.76 us
    pallas_call x1, Pallas kernels, per_device(): pl.pallas_call(functools.partial(second_kernel, line, even_ring), out_sha...  0.59 us
    ppermute x1, starting transfers between devices, per_device(): halo = lax.ppermute(message, 'azim', [(0, 1), (1, 0)])  0.56 us
  transfers between devices with their start and end apart: 3, of which 1 were waited for; matrix products, arithmetic and copies ran while one was open for 0% of the time, Pallas kernels for 19%

profile of v2, /device:TPU:0, one launch (start us, length us, event | category | flops | bytes accessed | tf_op | source)
XLA Modules:
  0.0 23.6 jit_solution(8076795825400394619)
XLA Ops:
  0.0 2.8 %first.1 = (bf16[128,128]{1,0:T(8,128)(2,1)S(1)}, f32[8,128]{1,0:T(8,128)S(1)}, bf16[592,128]{1,0:T(8,128)(2,1)S(1)}, f32[7,8,8,8,128]{4,3,2,1,0:T(8,128)S(1)}, bf16[4096,256]{1,0:T(8,128)(2,1)S(1)}) custom-call(bf16[7,512,128]{2,1,0:T(8,128)(2,1)} %fields_hbm.1, s32[1,128]{1,0:T(1,128)} %emap_hbm.1, f32[3,128]{1,0:T(4,128)} %metric_hbm.1, ...), custom_call_target="tpu_custom_call" | custom-call | tf_op jit(solution)/shard_map/first/pallas_call | solution.py:831
  2.8 0.6 %collective-permute-start = (bf16[592,128]{1,0:T(8,128)(2,1)S(1)}, bf16[592,128]{1,0:T(8,128)(2,1)S(1)}, u32[]{:S(2)}, u32[]{:S(2)}) collective-permute-start(bf16[592,128]{1,0:T(8,128)(2,1)S(1)} %get-tuple-element.19), channel_id=1, source_target_pairs={{0,1},{1,0},{2,3},{3,2},{4,5},{5,4},{6,7},{7,6},{8,9},{9,8},{10,11... | collective-permute-start | bytes 454664 | tf_op jit(solution)/shard_map/ppermute | solution.py:854
  4.0 0.4 %collective-permute-done.halo_ref = bf16[592,128]{1,0:T(8,128)(2,1)S(1)} collective-permute-done((bf16[592,128]{1,0:T(8,128)(2,1)S(1)}, bf16[592,128]{1,0:T(8,128)(2,1)S(1)}, u32[]{:S(2)}, u32[]{:S(2)}) %collective-permute-start) | collective-permute-done | bytes 151584 | tf_op jit(solution)/shard_map/ppermute | solution.py:854
  4.3 0.6 %second.1 = (f32[7,8,10,8,128]{4,3,2,1,0:T(8,128)S(1)}, f32[2,8,8,128]{3,2,1,0:T(8,128)S(1)}, f32[24,128]{1,0:T(8,128)S(1)}, bf16[400,128]{1,0:T(8,128)(2,1)S(1)}, bf16[400,128]{1,0:T(8,128)(2,1)S(1)}) custom-call(f32[7,8,8,8,128]{4,3,2,1,0:T(8,128)S(1)} %get-tuple-element.17.coarse_ref, f32[8,128]{1,0:T(8,128)S(1)} %get-tuple-element.18.metric_ref, ...), custom_call_target="tpu_custom_call" | custom-call | tf_op jit(solution)/shard_map/second/pallas_call | solution.py:863
  4.9 2.9 %collective-permute-start.1 = (bf16[400,128]{1,0:T(8,128)(2,1)S(1)}, bf16[400,128]{1,0:T(8,128)(2,1)S(1)}, u32[]{:S(2)}, u32[]{:S(2)}) collective-permute-start(bf16[400,128]{1,0:T(8,128)(2,1)S(1)} %get-tuple-element.26), channel_id=1, source_target_pairs={{0,2},{2,0},{4,6},{6,4},{8,10},{10,8},{12,14},{14,12},{1,3},{3,1},... | collective-permute-start | bytes 307208 | tf_op jit(solution)/shard_map/ppermute | solution.py:883
  7.8 3.6 %collective-permute-start.2 = (bf16[400,128]{1,0:T(8,128)(2,1)S(1)}, bf16[400,128]{1,0:T(8,128)(2,1)S(1)}, u32[]{:S(2)}, u32[]{:S(2)}) collective-permute-start(bf16[400,128]{1,0:T(8,128)(2,1)S(1)} %get-tuple-element.27), channel_id=1, source_target_pairs={{2,4},{4,2},{6,8},{8,6},{10,12},{12,10},{14,0},{0,14},{3,5},{5,3},... | collective-permute-start | bytes 307208 | tf_op jit(solution)/shard_map/ppermute | solution.py:884
  11.4 4.5 %third.1 = (f32[4,4,8,128,256]{4,3,2,1,0:T(8,128)S(1)}, bf16[2304,256]{1,0:T(8,128)(2,1)S(1)}) custom-call(f32[7,8,10,8,128]{4,3,2,1,0:T(8,128)S(1)} %get-tuple-element.20.ext_ref, bf16[4096,256]{1,0:T(8,128)(2,1)S(1)} %get-tuple-element.21.const_ref, bf16[2304,256]{1,0:T(8,128)(2,1)} %constant.5.clone.later_hbm), custom_call_target="tpu_custom_call" | custom-call | flops 4000000000 | bytes 20000000 | tf_op jit(solution)/shard_map/third/pallas_call | solution.py:889
  15.9 0.0 collective-permute-done.1.ra_ref
  15.9 0.0 collective-permute-done.2.rb_ref
  15.9 7.7 %fourth.1 = f32[1,128]{1,0:T(1,128)} custom-call(f32[1]{0:T(128)S(6)} %copy.7.inv_ref, f32[4,4,8,128,256]{4,3,2,1,0:T(8,128)S(1)} %get-tuple-element.22.gs_ref, f32[7,8,10,8,128]{4,3,2,1,0:T(8,128)S(1)} %get-tuple-element.20.ext_ref, f32[2,8,8,128]{3,2,1,0:T(8,128)S(1)} %get-tuple-element.23.ends_ref, f32[24,128]{1,0:T(8,128)S(1)} %get-tuple-element.24.table_ref, ...), custom_call_target="tpu_custom_call" | custom-call | tf_op jit(solution)/shard_map/fourth/pallas_call | solution.py:906
Async XLA Ops:
  2.8 1.6 %collective-permute-start = (bf16[592,128]{1,0:T(8,128)(2,1)S(1)}, bf16[592,128]{1,0:T(8,128)(2,1)S(1)}, u32[]{:S(2)}, u32[]{:S(2)}) collective-permute-start(bf16[592,128]{1,0:T(8,128)(2,1)S(1)} %get-tuple-element.19), channel_id=1, source_target_pairs={{0,1},{1,0},{2,3},{3,2},{4,5},{5,4},{6,7},{7,6},{8,9},{9,8},{10,11... | collective-permute-start | bytes 454664 | tf_op jit(solution)/shard_map/ppermute | solution.py:854
  4.9 11.0 %collective-permute-start.1 = (bf16[400,128]{1,0:T(8,128)(2,1)S(1)}, bf16[400,128]{1,0:T(8,128)(2,1)S(1)}, u32[]{:S(2)}, u32[]{:S(2)}) collective-permute-start(bf16[400,128]{1,0:T(8,128)(2,1)S(1)} %get-tuple-element.26), channel_id=1, source_target_pairs={{0,2},{2,0},{4,6},{6,4},{8,10},{10,8},{12,14},{14,12},{1,3},{3,1},... | collective-permute-start | bytes 307208 | tf_op jit(solution)/shard_map/ppermute | solution.py:883
  7.8 8.1 %collective-permute-start.2 = (bf16[400,128]{1,0:T(8,128)(2,1)S(1)}, bf16[400,128]{1,0:T(8,128)(2,1)S(1)}, u32[]{:S(2)}, u32[]{:S(2)}) collective-permute-start(bf16[400,128]{1,0:T(8,128)(2,1)S(1)} %get-tuple-element.27), channel_id=1, source_target_pairs={{2,4},{4,2},{6,8},{8,6},{10,12},{12,10},{14,0},{0,14},{3,5},{5,3},... | collective-permute-start | bytes 307208 | tf_op jit(solution)/shard_map/ppermute | solution.py:884

commit v3 on v2

--- a/solution.py
+++ b/solution.py
@@ -259,9 +259,8 @@
     slots_ref,
     metric_out,
     msg_ref,
-    coarse_ref,
+    fields,
     table_ref,
-    fields,
     emap,
     metric,
     sem,
@@ -293,9 +292,15 @@
     iy = positions((1, 1, count))[1]
     for f, copy in zip(order, large):
         copy.wait()
-        values = dot(fields[f], slots, True).reshape(NI, NI, NI, count)
-        coarse_ref[f] = values
-        face = jnp.where(iy == 0, values[:, 0], values[:, NI - 1])
+        if f in (3, 5):
+            values = dot(fields[f], slots, True).reshape(NI, NI, NI, count)
+            first, last = values[:, 0], values[:, NI - 1]
+        else:
+            planes = fields[f].reshape(NI, NI, NI, count)
+            planes = jnp.concatenate([planes[:, 0], planes[:, NI - 1]], axis=0)
+            planes = dot(planes.reshape(2 * NI * NI, count), slots, True)
+            first, last = rows3(planes[0:64]), rows3(planes[64:128])
+        face = jnp.where(iy == 0, first, last)
         msg_ref[f * 64 : f * 64 + 64, :] = rows2(face).astype(BF)
         if f in (3, 5):
             low, high = end_lines(line, [values[:, b] for b in range(NI)], EZ)
@@ -303,6 +308,13 @@
             msg_ref[at : at + 64, :] = rows2(jnp.where(iy == 0, low, high)).astype(BF)
     for copy in tables_copies:
         copy.wait()
+
+
+def own_kernel(fields_ref, slots_ref, coarse_ref):
+    count = fields_ref.shape[-1]
+    for f in range(7):
+        values = dot(fields_ref[f], slots_ref[...], True)
+        coarse_ref[f] = values.reshape(NI, NI, NI, count)
 
 
 def from_azim(x, iy):
@@ -440,7 +452,7 @@
                 gs_ref[pair, q, sector ^ FLIPS[q], :, 0:width] = dot(const_ref[rows, :], source)
         return carry
 
-    lax.fori_loop(0, 8, refine, 0)
+    lax.fori_loop(0, 8, refine, 0, unroll=2)
     for copy in copies:
         copy.wait()
 
@@ -470,6 +482,7 @@
     normal_y_ref,
     quad_ref,
     xt_ref,
+    nodal_ref,
 ):
     count = ext_ref.shape[-1]
     layer = EY * EZ
@@ -665,6 +678,8 @@
 
         def nodal(f, q, factor):
             g = unfold(parts_of(f, q, at, edge))
+            for s in range(8):
+                nodal_ref[kept(f - 3, q - 1), s, at, :] = g[s]
             return [g[s] * factor_ref[factor(s), at, :] for s in range(8)]
 
         def along_x(i, f):
@@ -768,7 +783,10 @@
         for i in range(3):
             total = unfold_half([linear_ref[i, s, at, :] for s in range(8)])
             for j in range(3):
-                slope = part(3 + i, 1 + j)
+                if i == j:
+                    slope = part(3 + i, 1 + j)
+                else:
+                    slope = [nodal_ref[kept(i, j), side * 4 + s, at, :] for s in range(4)]
                 total = [total[s] - base[j][s] * slope[s] for s in range(4)]
                 if i == j:
                     more = [slope[s] * metric[i] for s in range(4)]
@@ -797,6 +815,10 @@
     out_ref[...] = moved[0:1] + moved[1:2] + moved[2:3]
 
 
+def kept(component, axis):
+    return component * 2 + (axis if axis < component else axis - 1)
+
+
 def unfold4(parts):
     plus0, minus0 = parts[0] + parts[1], parts[0] - parts[1]
     plus1, minus1 = parts[2] + parts[3], parts[2] - parts[3]
@@ -828,19 +850,18 @@
         pltpu.with_memory_space_constraint(item, pltpu.HBM)
         for item in (fields, elem_map, metric, jnp.asarray(refine), jnp.asarray(const))
     ]
-    slots, local_metric, message, coarse, refine = pl.pallas_call(
+    slots, local_metric, message, near_fields, refine = pl.pallas_call(
         functools.partial(first_kernel, line),
         out_shape=(
             struct((count, count), BF),
             struct((8, count)),
             struct((9 * 64 + 16, count), BF),
-            struct((7, NI, NI, NI, count)),
+            struct(fields.shape, BF),
             struct(refine.shape, BF),
         ),
         in_specs=[hbm] * 4,
         out_specs=(vmem,) * 5,
         scratch_shapes=[
-            pltpu.VMEM(fields.shape, BF),
             pltpu.VMEM(elem_map.shape, jnp.int32),
             pltpu.VMEM(metric.shape, F32),
             pltpu.SemaphoreType.DMA((17,)),
@@ -848,6 +869,18 @@
         compiler_params=params(6),
         name="first",
     )(*inputs[:4])
+
+    coarse = pl.pallas_call(
+        own_kernel,
+        out_shape=struct((7, NI, NI, NI, count)),
+        in_specs=[vmem] * 2,
+        out_specs=vmem,
+        compiler_params=params(6),
+        cost_estimate=pl.CostEstimate(
+            flops=2 * fields.size * count, bytes_accessed=3 * 10**6, transcendentals=0
+        ),
+        name="own",
+    )(near_fields, slots)
 
     azim = lax.axis_size("azim")
     if azim == 2:
@@ -919,6 +952,7 @@
             pltpu.VMEM((2, 4, ROWS, count), F32),
             pltpu.VMEM((ROWS, count), F32),
             pltpu.VMEM((PAIRS, 8, 48, 2 * count), BF),
+            pltpu.VMEM((6, 8, ROWS, count), F32),
         ],
         compiler_params=params(20),
         name="fourth",

time: 23.8 us -> 22.3 us (0.937)
  Pallas kernels: 15.5 us -> 14.5 us
  waiting for transfers between devices: 0.37 us -> 0.03 us
    pallas_call x1, Pallas kernels: 4.5 us -> 3.79 us  [per_device(): pl.pallas_call(third_kernel, out_shape=(struct((PAIRS, 4, 8, ROWS, 2 * co...]
    pallas_call x1, Pallas kernels: 7.67 us -> 7.2 us  [per_device(): pl.pallas_call(functools.partial(fourth_kernel, ends_value, weights, even...]
    pallas_call x0 -> x1, Pallas kernels: none -> 0.4 us  [per_device(): pl.pallas_call(own_kernel, out_shape=struct((7, NI, NI, NI, count)), in_s...]
    ppermute x1, waiting for transfers between devices: 0.36 us -> 0.01 us  [per_device(): halo = lax.ppermute(message, 'azim', [(0, 1), (1, 0)])]
    pallas_call x1, Pallas kernels: 2.76 us -> 2.5 us  [per_device(): pl.pallas_call(functools.partial(first_kernel, line), out_shape=(struct((...]
  transfers between devices with their start and end apart: 3 -> 3, of which waited for: 1 -> 0; matrix products, arithmetic and copies ran while one was open for 0% -> 0% of each run, Pallas kernels for 19% -> 19%
where the time goes in v3:
time: 22.3 us; the launch traced here: 22.2 us
  Pallas kernels  14.5 us (65%)
  starting transfers between devices  6.98 us (31%)
  between operations  0.7 us (3%)
    pallas_call x1, Pallas kernels, per_device(): pl.pallas_call(functools.partial(fourth_kernel, ends_value, weights, even...  7.2 us
    pallas_call x1, Pallas kernels, per_device(): pl.pallas_call(third_kernel, out_shape=(struct((PAIRS, 4, 8, ROWS, 2 * co...  3.79 us
    ppermute x1, starting transfers between devices, per_device(): got_b = lax.ppermute(to_b, 'strm', far)  3.58 us
    ppermute x1, starting transfers between devices, per_device(): got_a = lax.ppermute(to_a, 'strm', near)  2.85 us
    pallas_call x1, Pallas kernels, per_device(): pl.pallas_call(functools.partial(first_kernel, line), out_shape=(struct((...  2.5 us
    pallas_call x1, Pallas kernels, per_device(): pl.pallas_call(functools.partial(second_kernel, line, even_ring), out_sha...  0.6 us
    ppermute x1, starting transfers between devices, per_device(): halo = lax.ppermute(message, 'azim', [(0, 1), (1, 0)])  0.56 us
  transfers between devices with their start and end apart: 3, of which 0 were waited for; matrix products, arithmetic and copies ran while one was open for 0% of the time, Pallas kernels for 19%

profile of v3, /device:TPU:0, one launch (start us, length us, event | category | flops | bytes accessed | tf_op | source)
XLA Modules:
  0.0 22.2 jit_solution(10793337501768586705)
XLA Ops:
  0.0 2.5 %first.1 = (bf16[128,128]{1,0:T(8,128)(2,1)S(1)}, f32[8,128]{1,0:T(8,128)S(1)}, bf16[592,128]{1,0:T(8,128)(2,1)S(1)}, bf16[7,512,128]{2,1,0:T(8,128)(2,1)S(1)}, bf16[4096,256]{1,0:T(8,128)(2,1)S(1)}) custom-call(bf16[7,512,128]{2,1,0:T(8,128)(2,1)} %fields_hbm.1, s32[1,128]{1,0:T(1,128)} %emap_hbm.1, f32[3,128]{1,0:T(4,128)} %metric_hbm.1, ...), custom_call_target="tpu_custom_call" | custom-call | tf_op jit(solution)/shard_map/first/pallas_call | solution.py:853
  2.5 0.6 %collective-permute-start = (bf16[592,128]{1,0:T(8,128)(2,1)S(1)}, bf16[592,128]{1,0:T(8,128)(2,1)S(1)}, u32[]{:S(2)}, u32[]{:S(2)}) collective-permute-start(bf16[592,128]{1,0:T(8,128)(2,1)S(1)} %get-tuple-element.20), channel_id=1, source_target_pairs={{0,1},{1,0},{2,3},{3,2},{4,5},{5,4},{6,7},{7,6},{8,9},{9,8},{10,11... | collective-permute-start | bytes 454664 | tf_op jit(solution)/shard_map/ppermute | solution.py:887
  3.7 0.4 %own.1.coarse_ref = f32[7,8,8,8,128]{4,3,2,1,0:T(8,128)S(1)} custom-call(bf16[7,512,128]{2,1,0:T(8,128)(2,1)S(1)} %get-tuple-element.17.fields_ref, bf16[128,128]{1,0:T(8,128)(2,1)S(1)} %get-tuple-element.18.slots_ref), custom_call_target="tpu_custom_call" | custom-call | flops 117440512 | bytes 3000000 | tf_op jit(solution)/shard_map/own/pallas_call | solution.py:873
  4.1 0.0 collective-permute-done.halo_ref
  4.1 0.6 %second.1 = (f32[7,8,10,8,128]{4,3,2,1,0:T(8,128)S(1)}, f32[2,8,8,128]{3,2,1,0:T(8,128)S(1)}, f32[24,128]{1,0:T(8,128)S(1)}, bf16[400,128]{1,0:T(8,128)(2,1)S(1)}, bf16[400,128]{1,0:T(8,128)(2,1)S(1)}) custom-call(f32[7,8,8,8,128]{4,3,2,1,0:T(8,128)S(1)} %own.1.coarse_ref, f32[8,128]{1,0:T(8,128)S(1)} %get-tuple-element.19.metric_ref, ...), custom_call_target="tpu_custom_call" | custom-call | tf_op jit(solution)/shard_map/second/pallas_call | solution.py:896
  4.7 2.9 %collective-permute-start.1 = (bf16[400,128]{1,0:T(8,128)(2,1)S(1)}, bf16[400,128]{1,0:T(8,128)(2,1)S(1)}, u32[]{:S(2)}, u32[]{:S(2)}) collective-permute-start(bf16[400,128]{1,0:T(8,128)(2,1)S(1)} %get-tuple-element.26), channel_id=1, source_target_pairs={{0,2},{2,0},{4,6},{6,4},{8,10},{10,8},{12,14},{14,12},{1,3},{3,1},... | collective-permute-start | bytes 307208 | tf_op jit(solution)/shard_map/ppermute | solution.py:916
  7.6 3.6 %collective-permute-start.2 = (bf16[400,128]{1,0:T(8,128)(2,1)S(1)}, bf16[400,128]{1,0:T(8,128)(2,1)S(1)}, u32[]{:S(2)}, u32[]{:S(2)}) collective-permute-start(bf16[400,128]{1,0:T(8,128)(2,1)S(1)} %get-tuple-element.27), channel_id=1, source_target_pairs={{2,4},{4,2},{6,8},{8,6},{10,12},{12,10},{14,0},{0,14},{3,5},{5,3},... | collective-permute-start | bytes 307208 | tf_op jit(solution)/shard_map/ppermute | solution.py:917
  11.2 3.8 %third.1 = (f32[4,4,8,128,256]{4,3,2,1,0:T(8,128)S(1)}, bf16[2304,256]{1,0:T(8,128)(2,1)S(1)}) custom-call(f32[7,8,10,8,128]{4,3,2,1,0:T(8,128)S(1)} %get-tuple-element.21.ext_ref, bf16[4096,256]{1,0:T(8,128)(2,1)S(1)} %get-tuple-element.22.const_ref, bf16[2304,256]{1,0:T(8,128)(2,1)} %constant.5.clone.later_hbm), custom_call_target="tpu_custom_call" | custom-call | flops 4000000000 | bytes 20000000 | tf_op jit(solution)/shard_map/third/pallas_call | solution.py:922
  15.0 0.0 collective-permute-done.1.ra_ref
  15.0 0.0 collective-permute-done.2.rb_ref
  15.0 7.2 %fourth.1 = f32[1,128]{1,0:T(1,128)} custom-call(f32[1]{0:T(128)S(6)} %copy.7.inv_ref, f32[4,4,8,128,256]{4,3,2,1,0:T(8,128)S(1)} %get-tuple-element.23.gs_ref, f32[7,8,10,8,128]{4,3,2,1,0:T(8,128)S(1)} %get-tuple-element.21.ext_ref, f32[2,8,8,128]{3,2,1,0:T(8,128)S(1)} %get-tuple-element.24.ends_ref, f32[24,128]{1,0:T(8,128)S(1)} %get-tuple-element.25.table_ref, ...), custom_call_target="tpu_custom_call" | custom-call | tf_op jit(solution)/shard_map/fourth/pallas_call | solution.py:939
Async XLA Ops:
  2.5 1.6 %collective-permute-start = (bf16[592,128]{1,0:T(8,128)(2,1)S(1)}, bf16[592,128]{1,0:T(8,128)(2,1)S(1)}, u32[]{:S(2)}, u32[]{:S(2)}) collective-permute-start(bf16[592,128]{1,0:T(8,128)(2,1)S(1)} %get-tuple-element.20), channel_id=1, source_target_pairs={{0,1},{1,0},{2,3},{3,2},{4,5},{5,4},{6,7},{7,6},{8,9},{9,8},{10,11... | collective-permute-start | bytes 454664 | tf_op jit(solution)/shard_map/ppermute | solution.py:887
  4.7 10.2 %collective-permute-start.1 = (bf16[400,128]{1,0:T(8,128)(2,1)S(1)}, bf16[400,128]{1,0:T(8,128)(2,1)S(1)}, u32[]{:S(2)}, u32[]{:S(2)}) collective-permute-start(bf16[400,128]{1,0:T(8,128)(2,1)S(1)} %get-tuple-element.26), channel_id=1, source_target_pairs={{0,2},{2,0},{4,6},{6,4},{8,10},{10,8},{12,14},{14,12},{1,3},{3,1},... | collective-permute-start | bytes 307208 | tf_op jit(solution)/shard_map/ppermute | solution.py:916
  7.6 7.4 %collective-permute-start.2 = (bf16[400,128]{1,0:T(8,128)(2,1)S(1)}, bf16[400,128]{1,0:T(8,128)(2,1)S(1)}, u32[]{:S(2)}, u32[]{:S(2)}) collective-permute-start(bf16[400,128]{1,0:T(8,128)(2,1)S(1)} %get-tuple-element.27), channel_id=1, source_target_pairs={{2,4},{4,2},{6,8},{8,6},{10,12},{12,10},{14,0},{0,14},{3,5},{5,3},... | collective-permute-start | bytes 307208 | tf_op jit(solution)/shard_map/ppermute | solution.py:917

commit v4 on v3

--- a/solution.py
+++ b/solution.py
@@ -17,7 +17,8 @@
 HI = NI // 2
 HO = NO // 2
 ROWS = 128
-SEAM_ROWS = ROWS + 3 * 32
+SEAM_ROWS = ROWS + 2 * 32
+GROUPS = sorted({row // 8 * 8 for row in range(HO**3) if row % (HO * HO) < HO})
 EXT = NI + 2
 SEAM = EXT * NI
 BF = jnp.bfloat16
@@ -125,7 +126,7 @@
             ends_of.append(added)
         refine.append(two_terms(np.concatenate(blocks)))
         rows = [pad_rows(ends_of[1], ROWS)]
-        rows += [pad_rows(ends_of[q][: HO * HO], 32) for q in (0, 2, 3)]
+        rows += [pad_rows(ends_of[q][: HO * HO], 32) for q in (2, 3)]
         seams.append(np.pad(two_terms(np.concatenate(rows)), ((0, 0), (0, ROWS - 96))))
     refine = np.stack(refine)
     seams = [np.concatenate(seams[2 * i : 2 * i + 2], axis=1) for i in range(4)]
@@ -156,11 +157,13 @@
             lift_x.append(pad_rows(face.reshape(HO * HO, -1), 32))
             spread = np.zeros((HO, HO, HO, 2 * SEAM))
             spread[:, 0] = face
-            lift_y.append(pad_rows(spread.reshape(HO**3, -1), ROWS))
+            spread = pad_rows(spread.reshape(HO**3, -1), ROWS)
+            lift_y.append(np.concatenate([spread[at : at + 8] for at in GROUPS]))
 
     def one_term(parts):
         matrix = np.concatenate(parts)
-        return np.pad(matrix, ((0, 0), (0, 2 * ROWS - matrix.shape[1]))).astype(jnp.bfloat16)
+        edge = 2 * ROWS - matrix.shape[1]
+        return np.pad(matrix, ((0, 0), (0, edge))).astype(jnp.bfloat16)
 
     refine = refine.reshape(-1, 2 * ROWS)
     const = np.concatenate(
@@ -172,7 +175,8 @@
         weights_in = slopes[end].copy()
         weights_in[[0, NO - 1]] = 0.0
         line.append(([float(v) for v in weights_in @ interp], float(slopes[end, far])))
-    ends = (float(slopes[0, 0]), float(slopes[NO - 1, NO - 1]))
+    ratio = [1.0 / float(both[0, NI] + sign * both[0, NI + 1]) for sign in (1.0, -1.0)]
+    ends = (float(slopes[0, 0]), float(slopes[NO - 1, NO - 1]), ratio)
     return refine, const, half_weights, (line, ends)
 
 
@@ -412,7 +416,55 @@
     ]
 
 
-def third_kernel(ext_ref, const_ref, later_hbm, gs_ref, later_ref, tmp_ref, xs_ref, sem):
+def row_kinds(count):
+    row = lax.broadcasted_iota(jnp.int32, (ROWS, count), 0)
+    return row, row < HO * HO, lax.rem(row, HO * HO) < HO, lax.rem(row, HO) == 0
+
+
+def line_of(source, at):
+    return source[at : at + 1]
+
+
+def row_tables(weights, table, factor_ref, quad_ref):
+    count = table.shape[-1]
+    row, a_edge, b_edge, c_edge = row_kinds(count)
+
+    def weight_of(index):
+        result = jnp.full((ROWS, count), weights[0], F32)
+        for i in range(1, HO):
+            result = jnp.where(index == i, weights[i], result)
+        return result
+
+    a_pos = lax.div(row, HO * HO)
+    b_pos = lax.rem(lax.div(row, HO), HO)
+    quad = weight_of(a_pos) * weight_of(b_pos) * weight_of(lax.rem(row, HO))
+    quad_ref[...] = jnp.where(row < HO**3, quad, 0.0)
+
+    def by_radius(at, side):
+        return jnp.where(c_edge, line_of(table, at + 1 + side), line_of(table, at))
+
+    for one in range(2):
+        for two in range(2):
+            at = one * 2 + two
+            factor_ref[at] = jnp.where(b_edge, by_radius(3 + 3 * one, two), by_radius(0, two))
+            factor_ref[4 + at] = by_radius(9, two)
+            factor_ref[8 + at] = jnp.where(b_edge, line_of(table, 13 + two), line_of(table, 12))
+
+
+def third_kernel(
+    weights,
+    ext_ref,
+    table_ref,
+    const_ref,
+    later_hbm,
+    gs_ref,
+    later_ref,
+    factor_ref,
+    quad_ref,
+    tmp_ref,
+    xs_ref,
+    sem,
+):
     count = ext_ref.shape[-1]
     width = HO * HI
     iz = positions((width, count))[2]
@@ -421,6 +473,7 @@
     copies = chunks(later_hbm, later_ref, sem)
     for copy in copies:
         copy.start()
+    row_tables(weights, table_ref[...], factor_ref, quad_ref)
     for f in range(7):
         pair, side = PLACE[f]
         lanes = slice(side * count, (side + 1) * count)
@@ -459,10 +512,11 @@
 
 def fourth_kernel(
     ends_value,
-    weights,
     even_ring,
     inv_ref,
     gs_ref,
+    factor_ref,
+    quad_ref,
     ext_ref,
     ends_ref,
     table_ref,
@@ -477,10 +531,9 @@
     edge_ref,
     vort_ref,
     linear_ref,
-    factor_ref,
+    edge_factor_ref,
     normal_x_ref,
     normal_y_ref,
-    quad_ref,
     xt_ref,
     nodal_ref,
 ):
@@ -488,7 +541,7 @@
     layer = EY * EZ
     even = is_even(even_ring)
     ix = positions((SEAM, count))[0]
-    end_low, end_high = ends_value
+    end_low, end_high, value_of_slope = ends_value
     seam_at = 0
     second_at = seam_at + 4 * SEAM_ROWS
     lift_x_at = second_at + 6 * ROWS
@@ -541,6 +594,8 @@
                     operand = jnp.concatenate(rows, axis=0).astype(BF)
                     xt_ref[pair, pa * 4 + pb * 2 + pc, :, lanes] = operand
 
+    first_nodes = lax.broadcasted_iota(jnp.int32, (32, 2 * count), 0) < HO * HO
+
     def refine_seam(pa, pb, pc):
         sector = pa * 4 + pb * 2 + pc
         at = seam_at + (sector // 2) * SEAM_ROWS
@@ -555,29 +610,19 @@
             )
             for q, slot in ((0, 0), (2, 1), (3, 2)):
                 if q or pair < PAIRS - 1:
+                    at = ROWS + 32 * (slot - 1) if q else 0
+                    more = added[at : at + 32]
+                    if q == 0:
+                        more = jnp.where(first_nodes[:, 0:width], more * value_of_slope[pa], 0.0)
                     target = sector ^ FLIPS[q]
                     edge_ref[pair, slot, target, :, 0:width] = (
-                        gs_ref[pair, q, target, 0:32, 0:width]
-                        + added[ROWS + 32 * slot : ROWS + 32 * slot + 32]
+                        gs_ref[pair, q, target, 0:32, 0:width] + more
                     )
 
     for sector in range(8):
         refine_seam(sector // 4, sector // 2 % 2, sector % 2)
 
-    row = lax.broadcasted_iota(jnp.int32, (ROWS, count), 0)
-    a_edge = row < HO * HO
-    b_edge = lax.rem(row, HO * HO) < HO
-    c_edge = lax.rem(row, HO) == 0
-
-    def weight_of(index):
-        result = jnp.full((ROWS, count), weights[0], F32)
-        for i in range(1, HO):
-            result = jnp.where(index == i, weights[i], result)
-        return result
-
-    a_pos = lax.div(row, HO * HO)
-    quad = weight_of(a_pos) * weight_of(lax.rem(lax.div(row, HO), HO)) * weight_of(lax.rem(row, HO))
-    quad_ref[...] = jnp.where(row < HO**3, quad, 0.0)
+    row, a_edge, b_edge, c_edge = row_kinds(count)
 
     table = table_ref[...]
     packed = blocks[9]
@@ -586,9 +631,6 @@
     at_low = 0.5 * (table + jnp.where(lane_ix == 0, theirs, roll(table, layer)))
     at_high = 0.5 * (table + jnp.where(lane_ix == 0, roll(table, -layer), theirs))
 
-    def line_of(source, at):
-        return source[at : at + 1]
-
     def by_radius(source, at, side):
         return jnp.where(c_edge, line_of(source, at + 1 + side), line_of(source, at))
 
@@ -596,15 +638,10 @@
         edge = at_low if one == 0 else at_high
         for two in range(2):
             at = one * 2 + two
-            factor_ref[at] = jnp.where(
-                b_edge, by_radius(table, 3 + 3 * one, two), by_radius(table, 0, two)
-            )
-            factor_ref[4 + at] = jnp.where(
-                a_edge, by_radius(edge, 9, two), by_radius(table, 9, two)
-            )
-            inside = jnp.where(b_edge, line_of(table, 13 + two), line_of(table, 12))
-            outside = jnp.where(b_edge, line_of(edge, 13 + two), line_of(edge, 12))
-            factor_ref[8 + at] = jnp.where(a_edge, outside, inside)
+            outside = by_radius(edge, 9, two)[0:32]
+            edge_factor_ref[at] = jnp.where(a_edge[0:32], outside, factor_ref[4 + at, 0:32, :])
+            outside = jnp.where(b_edge[0:32], line_of(edge, 13 + two), line_of(edge, 12))
+            edge_factor_ref[4 + at] = jnp.where(a_edge[0:32], outside, factor_ref[8 + at, 0:32, :])
 
     def with_added(parts):
         halves = []
@@ -646,15 +683,18 @@
         other = blocks[9][8 * i : 8 * i + 8] + factor[0] * near
         low, high = stream_added(own[0], own[NI - 1], other)
         azim.append(jnp.concatenate([rows2(own), low, high], axis=0))
-    lifted = lift(lift_y_at, 4 * ROWS, with_added(azim))
+    span = 8 * len(GROUPS)
+    lifted = lift(lift_y_at, 4 * span, with_added(azim))
     for one in range(2):
         edge = at_low if one == 0 else at_high
         for two in range(2):
             at = one * 2 + two
             scale = jnp.where(a_edge, by_radius(edge, 15, two), by_radius(table, 15, two))
             for i in range(2):
-                part = lifted[at * ROWS : (at + 1) * ROWS, i * count : (i + 1) * count]
-                normal_y_ref[i, at] = part * scale
+                for k, start in enumerate(GROUPS):
+                    rows = slice(at * span + 8 * k, at * span + 8 * k + 8)
+                    part = lifted[rows, i * count : (i + 1) * count]
+                    normal_y_ref[i, at, start : start + 8] = part * scale[start : start + 8]
 
     def parts_of(f, q, at, edge):
         pair, side = PLACE[f]
@@ -676,11 +716,16 @@
         on_b = lax.rem(rows, HO * HO) < HO
         on_c = lax.rem(rows, HO) == 0
 
+        def factor_at(which):
+            if edge and which >= 4:
+                return edge_factor_ref[which - 4, at, :]
+            return factor_ref[which, at, :]
+
         def nodal(f, q, factor):
             g = unfold(parts_of(f, q, at, edge))
             for s in range(8):
                 nodal_ref[kept(f - 3, q - 1), s, at, :] = g[s]
-            return [g[s] * factor_ref[factor(s), at, :] for s in range(8)]
+            return [g[s] * factor_at(factor(s)) for s in range(8)]
 
         def along_x(i, f):
             g = nodal(f, 1, lambda s: s % 4)
@@ -803,8 +848,8 @@
         return (energy[0] + energy[1]) + (energy[2] + energy[3])
 
     total = jnp.zeros((8, count), F32)
-    total = lax.fori_loop(0, 4, functools.partial(body, True), total)
-    total = lax.fori_loop(4, ROWS // 8, functools.partial(body, False), total)
+    total = lax.fori_loop(0, 4, functools.partial(body, True), total, unroll=2)
+    total = lax.fori_loop(4, ROWS // 8, functools.partial(body, False), total, unroll=2)
     weighted = jnp.sum(total, axis=0, keepdims=True)
     result = jnp.sqrt(weighted / 8.0) / float(ORDER_OUT**2)
     high, mid, low = split3(result)
@@ -919,11 +964,16 @@
         got_b = lax.ppermute(to_a, "strm", [(i, (i + 1) % streams) for i in range(streams)])
         got_a = lax.ppermute(to_b, "strm", [((i + 1) % streams, i) for i in range(streams)])
 
-    raw, const = pl.pallas_call(
-        third_kernel,
-        out_shape=(struct((PAIRS, 4, 8, ROWS, 2 * count)), struct(const.shape, BF)),
-        in_specs=[vmem, vmem, hbm],
-        out_specs=(vmem, vmem),
+    raw, const, factor, quad = pl.pallas_call(
+        functools.partial(third_kernel, weights),
+        out_shape=(
+            struct((PAIRS, 4, 8, ROWS, 2 * count)),
+            struct(const.shape, BF),
+            struct((12, ROWS, count)),
+            struct((ROWS, count)),
+        ),
+        in_specs=[vmem] * 3 + [hbm],
+        out_specs=(vmem,) * 4,
         scratch_shapes=[
             pltpu.VMEM((8, HO * HI * NI, count), F32),
             pltpu.VMEM((PAIRS, 8, ROWS, 2 * count), BF),
@@ -934,12 +984,12 @@
             flops=4 * 10**9, bytes_accessed=20 * 10**6, transcendentals=0
         ),
         name="third",
-    )(extended, refine, inputs[4])
+    )(extended, table, refine, inputs[4])
 
     result = pl.pallas_call(
-        functools.partial(fourth_kernel, ends_value, weights, even_ring),
+        functools.partial(fourth_kernel, ends_value, even_ring),
         out_shape=struct((1, count)),
-        in_specs=[pl.BlockSpec(memory_space=pltpu.SMEM)] + [vmem] * 9,
+        in_specs=[pl.BlockSpec(memory_space=pltpu.SMEM)] + [vmem] * 11,
         out_specs=vmem,
         scratch_shapes=[
             pltpu.VMEM((8, NI * NI, count), F32),
@@ -947,10 +997,9 @@
             pltpu.VMEM((PAIRS, 3, 8, 32, 2 * count), F32),
             pltpu.VMEM((3, 8, ROWS, count), BF),
             pltpu.VMEM((3, 8, ROWS, count), F32),
-            pltpu.VMEM((12, ROWS, count), F32),
+            pltpu.VMEM((8, 32, count), F32),
             pltpu.VMEM((2, 4, 32, count), F32),
             pltpu.VMEM((2, 4, ROWS, count), F32),
-            pltpu.VMEM((ROWS, count), F32),
             pltpu.VMEM((PAIRS, 8, 48, 2 * count), BF),
             pltpu.VMEM((6, 8, ROWS, count), F32),
         ],
@@ -959,6 +1008,8 @@
     )(
         inv_reynolds,
         raw,
+        factor,
+        quad,
         extended,
         ends,
         table,

time: 22.3 us -> 21.9 us (0.982)
  Pallas kernels: 14.5 us -> 14.1 us
    pallas_call x2, Pallas kernels: 11 us -> 10.6 us  [the longest x1 6.66 us: per_device(): pl.pallas_call(functools.partial(fourth_kernel, ends_value, even_ring), o...]
  transfers between devices with their start and end apart: 3 -> 3, of which waited for: 0 -> 0; matrix products, arithmetic and copies ran while one was open for 0% -> 0% of each run, Pallas kernels for 19% -> 20%
where the time goes in v4:
time: 21.9 us; the launch traced here: 21.8 us
  Pallas kernels  14.1 us (64%)
  starting transfers between devices  6.98 us (32%)
  between operations  0.7 us (3%)
    pallas_call x1, Pallas kernels, per_device(): pl.pallas_call(functools.partial(fourth_kernel, ends_value, even_ring), o...  6.66 us
    pallas_call x1, Pallas kernels, per_device(): pl.pallas_call(functools.partial(third_kernel, weights), out_shape=(struc...  3.94 us
    ppermute x1, starting transfers between devices, per_device(): got_b = lax.ppermute(to_b, 'strm', far)  3.58 us
    ppermute x1, starting transfers between devices, per_device(): got_a = lax.ppermute(to_a, 'strm', near)  2.85 us
    pallas_call x1, Pallas kernels, per_device(): pl.pallas_call(functools.partial(first_kernel, line), out_shape=(struct((...  2.5 us
    pallas_call x1, Pallas kernels, per_device(): pl.pallas_call(functools.partial(second_kernel, line, even_ring), out_sha...  0.6 us
    ppermute x1, starting transfers between devices, per_device(): halo = lax.ppermute(message, 'azim', [(0, 1), (1, 0)])  0.56 us
  transfers between devices with their start and end apart: 3, of which 0 were waited for; matrix products, arithmetic and copies ran while one was open for 0% of the time, Pallas kernels for 20%

profile of v4, /device:TPU:0, one launch (start us, length us, event | category | flops | bytes accessed | tf_op | source)
XLA Modules:
  0.0 21.8 jit_solution(87594086190664759)
XLA Ops:
  0.0 2.5 %first.1 = (bf16[128,128]{1,0:T(8,128)(2,1)S(1)}, f32[8,128]{1,0:T(8,128)S(1)}, bf16[592,128]{1,0:T(8,128)(2,1)S(1)}, bf16[7,512,128]{2,1,0:T(8,128)(2,1)S(1)}, bf16[4096,256]{1,0:T(8,128)(2,1)S(1)}) custom-call(bf16[7,512,128]{2,1,0:T(8,128)(2,1)} %fields_hbm.1, s32[1,128]{1,0:T(1,128)} %emap_hbm.1, f32[3,128]{1,0:T(4,128)} %metric_hbm.1, ...), custom_call_target="tpu_custom_call" | custom-call | tf_op jit(solution)/shard_map/first/pallas_call | solution.py:898
  2.5 0.6 %collective-permute-start = (bf16[592,128]{1,0:T(8,128)(2,1)S(1)}, bf16[592,128]{1,0:T(8,128)(2,1)S(1)}, u32[]{:S(2)}, u32[]{:S(2)}) collective-permute-start(bf16[592,128]{1,0:T(8,128)(2,1)S(1)} %get-tuple-element.22), channel_id=1, source_target_pairs={{0,1},{1,0},{2,3},{3,2},{4,5},{5,4},{6,7},{7,6},{8,9},{9,8},{10,11... | collective-permute-start | bytes 454664 | tf_op jit(solution)/shard_map/ppermute | solution.py:932
  3.7 0.4 %own.1.coarse_ref = f32[7,8,8,8,128]{4,3,2,1,0:T(8,128)S(1)} custom-call(bf16[7,512,128]{2,1,0:T(8,128)(2,1)S(1)} %get-tuple-element.19.fields_ref, bf16[128,128]{1,0:T(8,128)(2,1)S(1)} %get-tuple-element.20.slots_ref), custom_call_target="tpu_custom_call" | custom-call | flops 117440512 | bytes 3000000 | tf_op jit(solution)/shard_map/own/pallas_call | solution.py:918
  4.1 0.0 collective-permute-done.halo_ref
  4.1 0.6 %second.1 = (f32[7,8,10,8,128]{4,3,2,1,0:T(8,128)S(1)}, f32[2,8,8,128]{3,2,1,0:T(8,128)S(1)}, f32[24,128]{1,0:T(8,128)S(1)}, bf16[400,128]{1,0:T(8,128)(2,1)S(1)}, bf16[400,128]{1,0:T(8,128)(2,1)S(1)}) custom-call(f32[7,8,8,8,128]{4,3,2,1,0:T(8,128)S(1)} %own.1.coarse_ref, f32[8,128]{1,0:T(8,128)S(1)} %get-tuple-element.21.metric_ref, ...), custom_call_target="tpu_custom_call" | custom-call | tf_op jit(solution)/shard_map/second/pallas_call | solution.py:941
  4.7 2.9 %collective-permute-start.1 = (bf16[400,128]{1,0:T(8,128)(2,1)S(1)}, bf16[400,128]{1,0:T(8,128)(2,1)S(1)}, u32[]{:S(2)}, u32[]{:S(2)}) collective-permute-start(bf16[400,128]{1,0:T(8,128)(2,1)S(1)} %get-tuple-element.30), channel_id=1, source_target_pairs={{0,2},{2,0},{4,6},{6,4},{8,10},{10,8},{12,14},{14,12},{1,3},{3,1},... | collective-permute-start | bytes 307208 | tf_op jit(solution)/shard_map/ppermute | solution.py:961
  7.6 3.6 %collective-permute-start.2 = (bf16[400,128]{1,0:T(8,128)(2,1)S(1)}, bf16[400,128]{1,0:T(8,128)(2,1)S(1)}, u32[]{:S(2)}, u32[]{:S(2)}) collective-permute-start(bf16[400,128]{1,0:T(8,128)(2,1)S(1)} %get-tuple-element.31), channel_id=1, source_target_pairs={{2,4},{4,2},{6,8},{8,6},{10,12},{12,10},{14,0},{0,14},{3,5},{5,3},... | collective-permute-start | bytes 307208 | tf_op jit(solution)/shard_map/ppermute | solution.py:962
  11.2 3.9 %third.1 = (f32[4,4,8,128,256]{4,3,2,1,0:T(8,128)S(1)}, bf16[1856,256]{1,0:T(8,128)(2,1)S(1)}, f32[12,128,128]{2,1,0:T(8,128)S(1)}, f32[128,128]{1,0:T(8,128)S(1)}) custom-call(f32[7,8,10,8,128]{4,3,2,1,0:T(8,128)S(1)} %get-tuple-element.23.ext_ref, f32[24,128]{1,0:T(8,128)S(1)} %get-tuple-element.24.table_ref, ...), custom_call_target="tpu_custom_call" | custom-call | flops 4000000000 | bytes 20000000 | tf_op jit(solution)/shard_map/third/pallas_call | solution.py:967
  15.1 0.0 collective-permute-done.1.ra_ref
  15.1 0.0 collective-permute-done.2.rb_ref
  15.1 6.7 %fourth.1 = f32[1,128]{1,0:T(1,128)} custom-call(f32[1]{0:T(128)S(6)} %copy.7.inv_ref, f32[4,4,8,128,256]{4,3,2,1,0:T(8,128)S(1)} %get-tuple-element.26.gs_ref, f32[12,128,128]{2,1,0:T(8,128)S(1)} %get-tuple-element.27.factor_ref, f32[128,128]{1,0:T(8,128)S(1)} %get-tuple-element.28.quad_ref, f32[7,8,10,8,128]{4,3,2,1,0:T(8,128)S(1)} %get-tuple-element.23.ext_ref, ...), custom_call_target="tpu_custom_call" | custom-call | tf_op jit(solution)/shard_map/fourth/pallas_call | solution.py:989
Async XLA Ops:
  2.5 1.6 %collective-permute-start = (bf16[592,128]{1,0:T(8,128)(2,1)S(1)}, bf16[592,128]{1,0:T(8,128)(2,1)S(1)}, u32[]{:S(2)}, u32[]{:S(2)}) collective-permute-start(bf16[592,128]{1,0:T(8,128)(2,1)S(1)} %get-tuple-element.22), channel_id=1, source_target_pairs={{0,1},{1,0},{2,3},{3,2},{4,5},{5,4},{6,7},{7,6},{8,9},{9,8},{10,11... | collective-permute-start | bytes 454664 | tf_op jit(solution)/shard_map/ppermute | solution.py:932
  4.7 10.4 %collective-permute-start.1 = (bf16[400,128]{1,0:T(8,128)(2,1)S(1)}, bf16[400,128]{1,0:T(8,128)(2,1)S(1)}, u32[]{:S(2)}, u32[]{:S(2)}) collective-permute-start(bf16[400,128]{1,0:T(8,128)(2,1)S(1)} %get-tuple-element.30), channel_id=1, source_target_pairs={{0,2},{2,0},{4,6},{6,4},{8,10},{10,8},{12,14},{14,12},{1,3},{3,1},... | collective-permute-start | bytes 307208 | tf_op jit(solution)/shard_map/ppermute | solution.py:961
  7.6 7.5 %collective-permute-start.2 = (bf16[400,128]{1,0:T(8,128)(2,1)S(1)}, bf16[400,128]{1,0:T(8,128)(2,1)S(1)}, u32[]{:S(2)}, u32[]{:S(2)}) collective-permute-start(bf16[400,128]{1,0:T(8,128)(2,1)S(1)} %get-tuple-element.31), channel_id=1, source_target_pairs={{2,4},{4,2},{6,8},{8,6},{10,12},{12,10},{14,0},{0,14},{3,5},{5,3},... | collective-permute-start | bytes 307208 | tf_op jit(solution)/shard_map/ppermute | solution.py:962

commit v5 on v4

--- a/solution.py
+++ b/solution.py
@@ -279,23 +279,13 @@
     tables_copies = chunks(table_hbm, table_ref, sem.at[pl.ds(9, 8)])
     for copy in small + large + tables_copies:
         copy.start()
-    for copy in small:
+    for copy in small + large:
         copy.wait()
     local = lax.broadcasted_iota(jnp.int32, (count, count), 0)
     slots = (local == emap[...]).astype(F32).astype(BF)
     slots_ref[...] = slots
-    high, mid, low = split3(metric[...])
-    pad = jnp.zeros((7, count), F32)
-    stacked = jnp.concatenate([high.astype(F32), mid.astype(F32), low.astype(F32), pad], axis=0)
-    moved = dot(stacked.astype(BF), slots, True)
-    local = moved[0:3] + moved[3:6] + moved[6:9]
-    metric_out[...] = jnp.concatenate([local, jnp.zeros((5, count), F32)], axis=0)
-    high = local.astype(BF).astype(F32)
-    tail = jnp.concatenate([high, local - high, jnp.zeros((10, count), F32)], axis=0)
-    msg_ref[9 * 64 : 9 * 64 + 16, :] = tail.astype(BF)
     iy = positions((1, 1, count))[1]
-    for f, copy in zip(order, large):
-        copy.wait()
+    for f in order:
         if f in (3, 5):
             values = dot(fields[f], slots, True).reshape(NI, NI, NI, count)
             first, last = values[:, 0], values[:, NI - 1]
@@ -310,6 +300,15 @@
             low, high = end_lines(line, [values[:, b] for b in range(NI)], EZ)
             at = (7 + (f == 5)) * 64
             msg_ref[at : at + 64, :] = rows2(jnp.where(iy == 0, low, high)).astype(BF)
+    high, mid, low = split3(metric[...])
+    pad = jnp.zeros((7, count), F32)
+    stacked = jnp.concatenate([high.astype(F32), mid.astype(F32), low.astype(F32), pad], axis=0)
+    moved = dot(stacked.astype(BF), slots, True)
+    local = moved[0:3] + moved[3:6] + moved[6:9]
+    metric_out[...] = jnp.concatenate([local, jnp.zeros((5, count), F32)], axis=0)
+    high = local.astype(BF).astype(F32)
+    tail = jnp.concatenate([high, local - high, jnp.zeros((10, count), F32)], axis=0)
+    msg_ref[9 * 64 : 9 * 64 + 16, :] = tail.astype(BF)
     for copy in tables_copies:
         copy.wait()
 
@@ -547,20 +546,15 @@
     lift_x_at = second_at + 6 * ROWS
     lift_y_at = lift_x_at + ROWS
 
-    halves = []
-    for i in range(5):
-        rows = slice(i * SEAM, (i + 1) * SEAM)
+    def block(i):
+        rows = slice(i % 5 * SEAM, (i % 5 + 1) * SEAM)
         one = ra_ref[rows, :].astype(F32)
         two = rb_ref[rows, :].astype(F32)
         down = jnp.where(even, two, one)
         up = jnp.where(even, one, two)
-        halves.append(
-            (
-                jnp.where(ix == 0, down, roll(up, layer)),
-                jnp.where(ix == 0, roll(down, layer), up),
-            )
-        )
-    blocks = [item[0] for item in halves] + [item[1] for item in halves]
+        if i < 5:
+            return jnp.where(ix == 0, down, roll(up, layer))
+        return jnp.where(ix == 0, roll(down, layer), up)
 
     ix3 = positions((1, 1, count))[0]
     iz8 = positions((NI, count))[2]
@@ -573,10 +567,11 @@
 
     seam = {}
     tmp_ref[...] = jnp.zeros(tmp_ref.shape, F32)
-    for f in range(7):
+
+    def seam_operand(f):
         pair, side = PLACE[f]
         lanes = slice(side * count, (side + 1) * count)
-        halo = blocks[f].reshape(EXT, NI, count)
+        halo = block(f).reshape(EXT, NI, count)
         first, last = ext_ref[f, 0], ext_ref[f, NI - 1]
         low, high = stream_added(first, last, halo)
         if f in (4, 5):
@@ -596,36 +591,37 @@
 
     first_nodes = lax.broadcasted_iota(jnp.int32, (32, 2 * count), 0) < HO * HO
 
-    def refine_seam(pa, pb, pc):
-        sector = pa * 4 + pb * 2 + pc
+    def refine_seam(pair, sector):
         at = seam_at + (sector // 2) * SEAM_ROWS
-        matrix = const_ref[at : at + SEAM_ROWS, pc * ROWS : pc * ROWS + 2 * 48]
-        for pair in range(PAIRS):
-            width = 2 * count if pair < PAIRS - 1 else count
-            source = xt_ref[pair, sector, :, 0:width]
-            added = dot(matrix, jnp.concatenate([source, source], axis=0))
-            target = sector ^ 4
-            along_ref[pair, target, :, 0:width] = (
-                gs_ref[pair, 1, target, :, 0:width] + added[0:ROWS]
-            )
-            for q, slot in ((0, 0), (2, 1), (3, 2)):
-                if q or pair < PAIRS - 1:
-                    at = ROWS + 32 * (slot - 1) if q else 0
-                    more = added[at : at + 32]
-                    if q == 0:
-                        more = jnp.where(first_nodes[:, 0:width], more * value_of_slope[pa], 0.0)
-                    target = sector ^ FLIPS[q]
-                    edge_ref[pair, slot, target, :, 0:width] = (
-                        gs_ref[pair, q, target, 0:32, 0:width] + more
-                    )
-
-    for sector in range(8):
-        refine_seam(sector // 4, sector // 2 % 2, sector % 2)
+        half = sector % 2 * ROWS
+        matrix = const_ref[at : at + SEAM_ROWS, half : half + 2 * 48]
+        width = 2 * count if pair < PAIRS - 1 else count
+        source = xt_ref[pair, sector, :, 0:width]
+        added = dot(matrix, jnp.concatenate([source, source], axis=0))
+        target = sector ^ 4
+        along_ref[pair, target, :, 0:width] = gs_ref[pair, 1, target, :, 0:width] + added[0:ROWS]
+        for q, slot in ((0, 0), (2, 1), (3, 2)):
+            if q == 0 and pair == PAIRS - 1:
+                continue
+            if q == 0:
+                more = added[0:32] * value_of_slope[sector // 4]
+                more = jnp.where(first_nodes[:, 0:width], more, 0.0)
+            else:
+                more = added[ROWS + 32 * (slot - 1) : ROWS + 32 * slot]
+            target = sector ^ FLIPS[q]
+            edge_ref[pair, slot, target, :, 0:width] = gs_ref[pair, q, target, 0:32, 0:width] + more
+
+    for pair in range(PAIRS):
+        for f in range(7):
+            if PLACE[f][0] == pair:
+                seam_operand(f)
+        for sector in range(8):
+            refine_seam(pair, sector)
 
     row, a_edge, b_edge, c_edge = row_kinds(count)
 
     table = table_ref[...]
-    packed = blocks[9]
+    packed = block(9)
     theirs = packed[16:40] + packed[40:64]
     lane_ix = positions((24, count))[0]
     at_low = 0.5 * (table + jnp.where(lane_ix == 0, theirs, roll(table, layer)))
@@ -656,7 +652,7 @@
     stream = []
     for i in range(2):
         shared = jnp.where(ix == 0, end_high, end_low) * seam[4 + i]
-        stream.append(blocks[7 + i] + shared)
+        stream.append(block(7 + i) + shared)
     lifted = lift(lift_x_at, ROWS, with_added(stream))
     for one in range(2):
         for two in range(2):
@@ -674,13 +670,13 @@
     for i, f in enumerate((3, 5)):
         factor = jnp.where(iy3 == 0, end_high, end_low)
         values = ext_ref[f]
-        halo = blocks[f].reshape(EXT, NI, count)
+        halo = block(f).reshape(EXT, NI, count)
         near = jnp.where(
             iy3 == 0, values[:, 0] + values[:, NI], values[:, NI - 1] + values[:, NI + 1]
         )
         own = ends_ref[i] + factor * near
         near = jnp.where(iy2 == 0, halo[0] + halo[NI], halo[NI - 1] + halo[NI + 1])
-        other = blocks[9][8 * i : 8 * i + 8] + factor[0] * near
+        other = packed[8 * i : 8 * i + 8] + factor[0] * near
         low, high = stream_added(own[0], own[NI - 1], other)
         azim.append(jnp.concatenate([rows2(own), low, high], axis=0))
     span = 8 * len(GROUPS)

time: 21.9 us -> 21.6 us (0.986)
  Pallas kernels: 14.1 us -> 13.7 us
    pallas_call x1, Pallas kernels: 2.5 us -> 2.05 us  [per_device(): pl.pallas_call(functools.partial(first_kernel, line), out_shape=(struct((...]
where the time goes in v5:
time: 21.6 us; the launch traced here: 21.4 us
  Pallas kernels  13.7 us (63%)
  starting transfers between devices  6.98 us (32%)
  between operations  0.7 us (3%)
    pallas_call x1, Pallas kernels, per_device(): pl.pallas_call(functools.partial(fourth_kernel, ends_value, even_ring), o...  6.72 us
    pallas_call x1, Pallas kernels, per_device(): pl.pallas_call(functools.partial(third_kernel, weights), out_shape=(struc...  3.95 us
    ppermute x1, starting transfers between devices, per_device(): got_b = lax.ppermute(to_b, 'strm', far)  3.57 us
    ppermute x1, starting transfers between devices, per_device(): got_a = lax.ppermute(to_a, 'strm', near)  2.85 us
    pallas_call x1, Pallas kernels, per_device(): pl.pallas_call(functools.partial(first_kernel, line), out_shape=(struct((...  2.05 us
    pallas_call x1, Pallas kernels, per_device(): pl.pallas_call(functools.partial(second_kernel, line, even_ring), out_sha...  0.6 us
    ppermute x1, starting transfers between devices, per_device(): halo = lax.ppermute(message, 'azim', [(0, 1), (1, 0)])  0.56 us
  transfers between devices with their start and end apart: 3, of which 0 were waited for; matrix products, arithmetic and copies ran while one was open for 0% of the time, Pallas kernels for 20%

profile of v5, /device:TPU:0, one launch (start us, length us, event | category | flops | bytes accessed | tf_op | source)
XLA Modules:
  0.0 21.4 jit_solution(9922076762091560615)
XLA Ops:
  0.0 2.0 %first.1 = (bf16[128,128]{1,0:T(8,128)(2,1)S(1)}, f32[8,128]{1,0:T(8,128)S(1)}, bf16[592,128]{1,0:T(8,128)(2,1)S(1)}, bf16[7,512,128]{2,1,0:T(8,128)(2,1)S(1)}, bf16[4096,256]{1,0:T(8,128)(2,1)S(1)}) custom-call(bf16[7,512,128]{2,1,0:T(8,128)(2,1)} %fields_hbm.1, s32[1,128]{1,0:T(1,128)} %emap_hbm.1, f32[3,128]{1,0:T(4,128)} %metric_hbm.1, ...), custom_call_target="tpu_custom_call" | custom-call | tf_op jit(solution)/shard_map/first/pallas_call | solution.py:894
  2.1 0.6 %collective-permute-start = (bf16[592,128]{1,0:T(8,128)(2,1)S(1)}, bf16[592,128]{1,0:T(8,128)(2,1)S(1)}, u32[]{:S(2)}, u32[]{:S(2)}) collective-permute-start(bf16[592,128]{1,0:T(8,128)(2,1)S(1)} %get-tuple-element.22), channel_id=1, source_target_pairs={{0,1},{1,0},{2,3},{3,2},{4,5},{5,4},{6,7},{7,6},{8,9},{9,8},{10,11... | collective-permute-start | bytes 454664 | tf_op jit(solution)/shard_map/ppermute | solution.py:928
  3.3 0.4 %own.1.coarse_ref = f32[7,8,8,8,128]{4,3,2,1,0:T(8,128)S(1)} custom-call(bf16[7,512,128]{2,1,0:T(8,128)(2,1)S(1)} %get-tuple-element.19.fields_ref, bf16[128,128]{1,0:T(8,128)(2,1)S(1)} %get-tuple-element.20.slots_ref), custom_call_target="tpu_custom_call" | custom-call | flops 117440512 | bytes 3000000 | tf_op jit(solution)/shard_map/own/pallas_call | solution.py:914
  3.7 0.0 collective-permute-done.halo_ref
  3.7 0.6 %second.1 = (f32[7,8,10,8,128]{4,3,2,1,0:T(8,128)S(1)}, f32[2,8,8,128]{3,2,1,0:T(8,128)S(1)}, f32[24,128]{1,0:T(8,128)S(1)}, bf16[400,128]{1,0:T(8,128)(2,1)S(1)}, bf16[400,128]{1,0:T(8,128)(2,1)S(1)}) custom-call(f32[7,8,8,8,128]{4,3,2,1,0:T(8,128)S(1)} %own.1.coarse_ref, f32[8,128]{1,0:T(8,128)S(1)} %get-tuple-element.21.metric_ref, ...), custom_call_target="tpu_custom_call" | custom-call | tf_op jit(solution)/shard_map/second/pallas_call | solution.py:937
  4.3 2.9 %collective-permute-start.1 = (bf16[400,128]{1,0:T(8,128)(2,1)S(1)}, bf16[400,128]{1,0:T(8,128)(2,1)S(1)}, u32[]{:S(2)}, u32[]{:S(2)}) collective-permute-start(bf16[400,128]{1,0:T(8,128)(2,1)S(1)} %get-tuple-element.30), channel_id=1, source_target_pairs={{0,2},{2,0},{4,6},{6,4},{8,10},{10,8},{12,14},{14,12},{1,3},{3,1},... | collective-permute-start | bytes 307208 | tf_op jit(solution)/shard_map/ppermute | solution.py:957
  7.1 3.6 %collective-permute-start.2 = (bf16[400,128]{1,0:T(8,128)(2,1)S(1)}, bf16[400,128]{1,0:T(8,128)(2,1)S(1)}, u32[]{:S(2)}, u32[]{:S(2)}) collective-permute-start(bf16[400,128]{1,0:T(8,128)(2,1)S(1)} %get-tuple-element.31), channel_id=1, source_target_pairs={{2,4},{4,2},{6,8},{8,6},{10,12},{12,10},{14,0},{0,14},{3,5},{5,3},... | collective-permute-start | bytes 307208 | tf_op jit(solution)/shard_map/ppermute | solution.py:958
  10.7 3.9 %third.1 = (f32[4,4,8,128,256]{4,3,2,1,0:T(8,128)S(1)}, bf16[1856,256]{1,0:T(8,128)(2,1)S(1)}, f32[12,128,128]{2,1,0:T(8,128)S(1)}, f32[128,128]{1,0:T(8,128)S(1)}) custom-call(f32[7,8,10,8,128]{4,3,2,1,0:T(8,128)S(1)} %get-tuple-element.23.ext_ref, f32[24,128]{1,0:T(8,128)S(1)} %get-tuple-element.24.table_ref, ...), custom_call_target="tpu_custom_call" | custom-call | flops 4000000000 | bytes 20000000 | tf_op jit(solution)/shard_map/third/pallas_call | solution.py:963
  14.7 0.0 collective-permute-done.1.ra_ref
  14.7 0.0 collective-permute-done.2.rb_ref
  14.7 6.7 %fourth.1 = f32[1,128]{1,0:T(1,128)} custom-call(f32[1]{0:T(128)S(6)} %copy.7.inv_ref, f32[4,4,8,128,256]{4,3,2,1,0:T(8,128)S(1)} %get-tuple-element.26.gs_ref, f32[12,128,128]{2,1,0:T(8,128)S(1)} %get-tuple-element.27.factor_ref, f32[128,128]{1,0:T(8,128)S(1)} %get-tuple-element.28.quad_ref, f32[7,8,10,8,128]{4,3,2,1,0:T(8,128)S(1)} %get-tuple-element.23.ext_ref, ...), custom_call_target="tpu_custom_call" | custom-call | tf_op jit(solution)/shard_map/fourth/pallas_call | solution.py:985
Async XLA Ops:
  2.1 1.6 %collective-permute-start = (bf16[592,128]{1,0:T(8,128)(2,1)S(1)}, bf16[592,128]{1,0:T(8,128)(2,1)S(1)}, u32[]{:S(2)}, u32[]{:S(2)}) collective-permute-start(bf16[592,128]{1,0:T(8,128)(2,1)S(1)} %get-tuple-element.22), channel_id=1, source_target_pairs={{0,1},{1,0},{2,3},{3,2},{4,5},{5,4},{6,7},{7,6},{8,9},{9,8},{10,11... | collective-permute-start | bytes 454664 | tf_op jit(solution)/shard_map/ppermute | solution.py:928
  4.3 10.4 %collective-permute-start.1 = (bf16[400,128]{1,0:T(8,128)(2,1)S(1)}, bf16[400,128]{1,0:T(8,128)(2,1)S(1)}, u32[]{:S(2)}, u32[]{:S(2)}) collective-permute-start(bf16[400,128]{1,0:T(8,128)(2,1)S(1)} %get-tuple-element.30), channel_id=1, source_target_pairs={{0,2},{2,0},{4,6},{6,4},{8,10},{10,8},{12,14},{14,12},{1,3},{3,1},... | collective-permute-start | bytes 307208 | tf_op jit(solution)/shard_map/ppermute | solution.py:957
  7.1 7.5 %collective-permute-start.2 = (bf16[400,128]{1,0:T(8,128)(2,1)S(1)}, bf16[400,128]{1,0:T(8,128)(2,1)S(1)}, u32[]{:S(2)}, u32[]{:S(2)}) collective-permute-start(bf16[400,128]{1,0:T(8,128)(2,1)S(1)} %get-tuple-element.31), channel_id=1, source_target_pairs={{2,4},{4,2},{6,8},{8,6},{10,12},{12,10},{14,0},{0,14},{3,5},{5,3},... | collective-permute-start | bytes 307208 | tf_op jit(solution)/shard_map/ppermute | solution.py:958

commit v6 on v5

--- a/solution.py
+++ b/solution.py
@@ -504,7 +504,7 @@
                 gs_ref[pair, q, sector ^ FLIPS[q], :, 0:width] = dot(const_ref[rows, :], source)
         return carry
 
-    lax.fori_loop(0, 8, refine, 0, unroll=2)
+    lax.fori_loop(0, 8, refine, 0, unroll=4)
     for copy in copies:
         copy.wait()
 
@@ -777,7 +777,7 @@
         vorticity(pl.ds(start, chunk), start, False)
         return carry
 
-    lax.fori_loop(2, ROWS // chunk, vorticity_step, 0)
+    lax.fori_loop(2, ROWS // chunk, vorticity_step, 0, unroll=2)
 
     metric = [metric_ref[i : i + 1] for i in range(3)]
     inv = inv_ref[0]

time: 21.6 us -> 21.2 us (0.981)
  Pallas kernels: 13.7 us -> 13.2 us
  waiting for transfers between devices: 0.01 us -> 0.24 us
    pallas_call x1, Pallas kernels: 3.95 us -> 3.58 us  [per_device(): pl.pallas_call(functools.partial(third_kernel, weights), out_shape=(struc...]
    ppermute x1, waiting for transfers between devices: 0.01 us -> 0.23 us  [per_device(): got_b = lax.ppermute(to_b, 'strm', far)]
  transfers between devices with their start and end apart: 3 -> 3, of which waited for: 0 -> 1; matrix products, arithmetic and copies ran while one was open for 0% -> 0% of each run, Pallas kernels for 20% -> 19%
where the time goes in v6:
time: 21.2 us; the launch traced here: 21.1 us
  Pallas kernels  13.2 us (62%)
  starting transfers between devices  6.98 us (33%)
  between operations  0.7 us (3%)
  waiting for transfers between devices  0.24 us (1%)
    pallas_call x1, Pallas kernels, per_device(): pl.pallas_call(functools.partial(fourth_kernel, ends_value, even_ring), o...  6.55 us
    pallas_call x1, Pallas kernels, per_device(): pl.pallas_call(functools.partial(third_kernel, weights), out_shape=(struc...  3.58 us
    ppermute x1, starting transfers between devices, per_device(): got_b = lax.ppermute(to_b, 'strm', far)  3.57 us
    ppermute x1, starting transfers between devices, per_device(): got_a = lax.ppermute(to_a, 'strm', near)  2.85 us
    pallas_call x1, Pallas kernels, per_device(): pl.pallas_call(functools.partial(first_kernel, line), out_shape=(struct((...  2.05 us
    pallas_call x1, Pallas kernels, per_device(): pl.pallas_call(functools.partial(second_kernel, line, even_ring), out_sha...  0.6 us
    ppermute x1, starting transfers between devices, per_device(): halo = lax.ppermute(message, 'azim', [(0, 1), (1, 0)])  0.56 us
  transfers between devices with their start and end apart: 3, of which 1 were waited for; matrix products, arithmetic and copies ran while one was open for 0% of the time, Pallas kernels for 19%

profile of v6, /device:TPU:0, one launch (start us, length us, event | category | flops | bytes accessed | tf_op | source)
XLA Modules:
  0.0 21.1 jit_solution(9190951647087689685)
XLA Ops:
  0.0 2.0 %first.1 = (bf16[128,128]{1,0:T(8,128)(2,1)S(1)}, f32[8,128]{1,0:T(8,128)S(1)}, bf16[592,128]{1,0:T(8,128)(2,1)S(1)}, bf16[7,512,128]{2,1,0:T(8,128)(2,1)S(1)}, bf16[4096,256]{1,0:T(8,128)(2,1)S(1)}) custom-call(bf16[7,512,128]{2,1,0:T(8,128)(2,1)} %fields_hbm.1, s32[1,128]{1,0:T(1,128)} %emap_hbm.1, f32[3,128]{1,0:T(4,128)} %metric_hbm.1, ...), custom_call_target="tpu_custom_call" | custom-call | tf_op jit(solution)/shard_map/first/pallas_call | solution.py:894
  2.1 0.6 %collective-permute-start = (bf16[592,128]{1,0:T(8,128)(2,1)S(1)}, bf16[592,128]{1,0:T(8,128)(2,1)S(1)}, u32[]{:S(2)}, u32[]{:S(2)}) collective-permute-start(bf16[592,128]{1,0:T(8,128)(2,1)S(1)} %get-tuple-element.22), channel_id=1, source_target_pairs={{0,1},{1,0},{2,3},{3,2},{4,5},{5,4},{6,7},{7,6},{8,9},{9,8},{10,11... | collective-permute-start | bytes 454664 | tf_op jit(solution)/shard_map/ppermute | solution.py:928
  3.3 0.4 %own.1.coarse_ref = f32[7,8,8,8,128]{4,3,2,1,0:T(8,128)S(1)} custom-call(bf16[7,512,128]{2,1,0:T(8,128)(2,1)S(1)} %get-tuple-element.19.fields_ref, bf16[128,128]{1,0:T(8,128)(2,1)S(1)} %get-tuple-element.20.slots_ref), custom_call_target="tpu_custom_call" | custom-call | flops 117440512 | bytes 3000000 | tf_op jit(solution)/shard_map/own/pallas_call | solution.py:914
  3.7 0.0 collective-permute-done.halo_ref
  3.7 0.6 %second.1 = (f32[7,8,10,8,128]{4,3,2,1,0:T(8,128)S(1)}, f32[2,8,8,128]{3,2,1,0:T(8,128)S(1)}, f32[24,128]{1,0:T(8,128)S(1)}, bf16[400,128]{1,0:T(8,128)(2,1)S(1)}, bf16[400,128]{1,0:T(8,128)(2,1)S(1)}) custom-call(f32[7,8,8,8,128]{4,3,2,1,0:T(8,128)S(1)} %own.1.coarse_ref, f32[8,128]{1,0:T(8,128)S(1)} %get-tuple-element.21.metric_ref, ...), custom_call_target="tpu_custom_call" | custom-call | tf_op jit(solution)/shard_map/second/pallas_call | solution.py:937
  4.3 2.9 %collective-permute-start.1 = (bf16[400,128]{1,0:T(8,128)(2,1)S(1)}, bf16[400,128]{1,0:T(8,128)(2,1)S(1)}, u32[]{:S(2)}, u32[]{:S(2)}) collective-permute-start(bf16[400,128]{1,0:T(8,128)(2,1)S(1)} %get-tuple-element.30), channel_id=1, source_target_pairs={{0,2},{2,0},{4,6},{6,4},{8,10},{10,8},{12,14},{14,12},{1,3},{3,1},... | collective-permute-start | bytes 307208 | tf_op jit(solution)/shard_map/ppermute | solution.py:957
  7.1 3.6 %collective-permute-start.2 = (bf16[400,128]{1,0:T(8,128)(2,1)S(1)}, bf16[400,128]{1,0:T(8,128)(2,1)S(1)}, u32[]{:S(2)}, u32[]{:S(2)}) collective-permute-start(bf16[400,128]{1,0:T(8,128)(2,1)S(1)} %get-tuple-element.31), channel_id=1, source_target_pairs={{2,4},{4,2},{6,8},{8,6},{10,12},{12,10},{14,0},{0,14},{3,5},{5,3},... | collective-permute-start | bytes 307208 | tf_op jit(solution)/shard_map/ppermute | solution.py:958
  10.7 3.6 %third.1 = (f32[4,4,8,128,256]{4,3,2,1,0:T(8,128)S(1)}, bf16[1856,256]{1,0:T(8,128)(2,1)S(1)}, f32[12,128,128]{2,1,0:T(8,128)S(1)}, f32[128,128]{1,0:T(8,128)S(1)}) custom-call(f32[7,8,10,8,128]{4,3,2,1,0:T(8,128)S(1)} %get-tuple-element.23.ext_ref, f32[24,128]{1,0:T(8,128)S(1)} %get-tuple-element.24.table_ref, ...), custom_call_target="tpu_custom_call" | custom-call | flops 4000000000 | bytes 20000000 | tf_op jit(solution)/shard_map/third/pallas_call | solution.py:963
  14.3 0.0 collective-permute-done.1.ra_ref
  14.3 0.2 %collective-permute-done.2.rb_ref = bf16[400,128]{1,0:T(8,128)(2,1)S(1)} collective-permute-done((bf16[400,128]{1,0:T(8,128)(2,1)S(1)}, bf16[400,128]{1,0:T(8,128)(2,1)S(1)}, u32[]{:S(2)}, u32[]{:S(2)}) %collective-permute-start.2) | collective-permute-done | bytes 102432 | tf_op jit(solution)/shard_map/ppermute | solution.py:958
  14.5 6.6 %fourth.1 = f32[1,128]{1,0:T(1,128)} custom-call(f32[1]{0:T(128)S(6)} %copy.7.inv_ref, f32[4,4,8,128,256]{4,3,2,1,0:T(8,128)S(1)} %get-tuple-element.26.gs_ref, f32[12,128,128]{2,1,0:T(8,128)S(1)} %get-tuple-element.27.factor_ref, f32[128,128]{1,0:T(8,128)S(1)} %get-tuple-element.28.quad_ref, f32[7,8,10,8,128]{4,3,2,1,0:T(8,128)S(1)} %get-tuple-element.23.ext_ref, ...), custom_call_target="tpu_custom_call" | custom-call | tf_op jit(solution)/shard_map/fourth/pallas_call | solution.py:985
Async XLA Ops:
  2.1 1.6 %collective-permute-start = (bf16[592,128]{1,0:T(8,128)(2,1)S(1)}, bf16[592,128]{1,0:T(8,128)(2,1)S(1)}, u32[]{:S(2)}, u32[]{:S(2)}) collective-permute-start(bf16[592,128]{1,0:T(8,128)(2,1)S(1)} %get-tuple-element.22), channel_id=1, source_target_pairs={{0,1},{1,0},{2,3},{3,2},{4,5},{5,4},{6,7},{7,6},{8,9},{9,8},{10,11... | collective-permute-start | bytes 454664 | tf_op jit(solution)/shard_map/ppermute | solution.py:928
  4.3 10.0 %collective-permute-start.1 = (bf16[400,128]{1,0:T(8,128)(2,1)S(1)}, bf16[400,128]{1,0:T(8,128)(2,1)S(1)}, u32[]{:S(2)}, u32[]{:S(2)}) collective-permute-start(bf16[400,128]{1,0:T(8,128)(2,1)S(1)} %get-tuple-element.30), channel_id=1, source_target_pairs={{0,2},{2,0},{4,6},{6,4},{8,10},{10,8},{12,14},{14,12},{1,3},{3,1},... | collective-permute-start | bytes 307208 | tf_op jit(solution)/shard_map/ppermute | solution.py:957
  7.1 7.4 %collective-permute-start.2 = (bf16[400,128]{1,0:T(8,128)(2,1)S(1)}, bf16[400,128]{1,0:T(8,128)(2,1)S(1)}, u32[]{:S(2)}, u32[]{:S(2)}) collective-permute-start(bf16[400,128]{1,0:T(8,128)(2,1)S(1)} %get-tuple-element.31), channel_id=1, source_target_pairs={{2,4},{4,2},{6,8},{8,6},{10,12},{12,10},{14,0},{0,14},{3,5},{5,3},... | collective-permute-start | bytes 307208 | tf_op jit(solution)/shard_map/ppermute | solution.py:958

commit v7 on v6

--- a/solution.py
+++ b/solution.py
@@ -777,7 +777,7 @@
         vorticity(pl.ds(start, chunk), start, False)
         return carry
 
-    lax.fori_loop(2, ROWS // chunk, vorticity_step, 0, unroll=2)
+    lax.fori_loop(2, ROWS // chunk, vorticity_step, 0, unroll=3)
 
     metric = [metric_ref[i : i + 1] for i in range(3)]
     inv = inv_ref[0]

time: 21.2 us -> 21.3 us (level)
  no operation moved by 1% of the time
where the time goes in v7:
time: 21.3 us; the launch traced here: 21.1 us
  Pallas kernels  13.2 us (62%)
  starting transfers between devices  6.98 us (33%)
  between operations  0.7 us (3%)
  waiting for transfers between devices  0.24 us (1%)
    pallas_call x1, Pallas kernels, per_device(): pl.pallas_call(functools.partial(fourth_kernel, ends_value, even_ring), o...  6.57 us
    pallas_call x1, Pallas kernels, per_device(): pl.pallas_call(functools.partial(third_kernel, weights), out_shape=(struc...  3.58 us
    ppermute x1, starting transfers between devices, per_device(): got_b = lax.ppermute(to_b, 'strm', far)  3.57 us
    ppermute x1, starting transfers between devices, per_device(): got_a = lax.ppermute(to_a, 'strm', near)  2.85 us
    pallas_call x1, Pallas kernels, per_device(): pl.pallas_call(functools.partial(first_kernel, line), out_shape=(struct((...  2.05 us
    pallas_call x1, Pallas kernels, per_device(): pl.pallas_call(functools.partial(second_kernel, line, even_ring), out_sha...  0.6 us
    ppermute x1, starting transfers between devices, per_device(): halo = lax.ppermute(message, 'azim', [(0, 1), (1, 0)])  0.56 us
  transfers between devices with their start and end apart: 3, of which 1 were waited for; matrix products, arithmetic and copies ran while one was open for 0% of the time, Pallas kernels for 19%

profile of v7, /device:TPU:0, one launch (start us, length us, event | category | flops | bytes accessed | tf_op | source)
XLA Modules:
  0.0 21.1 jit_solution(3114565411989394383)
XLA Ops:
  0.0 2.0 %first.1 = (bf16[128,128]{1,0:T(8,128)(2,1)S(1)}, f32[8,128]{1,0:T(8,128)S(1)}, bf16[592,128]{1,0:T(8,128)(2,1)S(1)}, bf16[7,512,128]{2,1,0:T(8,128)(2,1)S(1)}, bf16[4096,256]{1,0:T(8,128)(2,1)S(1)}) custom-call(bf16[7,512,128]{2,1,0:T(8,128)(2,1)} %fields_hbm.1, s32[1,128]{1,0:T(1,128)} %emap_hbm.1, f32[3,128]{1,0:T(4,128)} %metric_hbm.1, ...), custom_call_target="tpu_custom_call" | custom-call | tf_op jit(solution)/shard_map/first/pallas_call | solution.py:894
  2.1 0.6 %collective-permute-start = (bf16[592,128]{1,0:T(8,128)(2,1)S(1)}, bf16[592,128]{1,0:T(8,128)(2,1)S(1)}, u32[]{:S(2)}, u32[]{:S(2)}) collective-permute-start(bf16[592,128]{1,0:T(8,128)(2,1)S(1)} %get-tuple-element.22), channel_id=1, source_target_pairs={{0,1},{1,0},{2,3},{3,2},{4,5},{5,4},{6,7},{7,6},{8,9},{9,8},{10,11... | collective-permute-start | bytes 454664 | tf_op jit(solution)/shard_map/ppermute | solution.py:928
  3.3 0.4 %own.1.coarse_ref = f32[7,8,8,8,128]{4,3,2,1,0:T(8,128)S(1)} custom-call(bf16[7,512,128]{2,1,0:T(8,128)(2,1)S(1)} %get-tuple-element.19.fields_ref, bf16[128,128]{1,0:T(8,128)(2,1)S(1)} %get-tuple-element.20.slots_ref), custom_call_target="tpu_custom_call" | custom-call | flops 117440512 | bytes 3000000 | tf_op jit(solution)/shard_map/own/pallas_call | solution.py:914
  3.7 0.0 collective-permute-done.halo_ref
  3.7 0.6 %second.1 = (f32[7,8,10,8,128]{4,3,2,1,0:T(8,128)S(1)}, f32[2,8,8,128]{3,2,1,0:T(8,128)S(1)}, f32[24,128]{1,0:T(8,128)S(1)}, bf16[400,128]{1,0:T(8,128)(2,1)S(1)}, bf16[400,128]{1,0:T(8,128)(2,1)S(1)}) custom-call(f32[7,8,8,8,128]{4,3,2,1,0:T(8,128)S(1)} %own.1.coarse_ref, f32[8,128]{1,0:T(8,128)S(1)} %get-tuple-element.21.metric_ref, ...), custom_call_target="tpu_custom_call" | custom-call | tf_op jit(solution)/shard_map/second/pallas_call | solution.py:937
  4.3 2.9 %collective-permute-start.1 = (bf16[400,128]{1,0:T(8,128)(2,1)S(1)}, bf16[400,128]{1,0:T(8,128)(2,1)S(1)}, u32[]{:S(2)}, u32[]{:S(2)}) collective-permute-start(bf16[400,128]{1,0:T(8,128)(2,1)S(1)} %get-tuple-element.30), channel_id=1, source_target_pairs={{0,2},{2,0},{4,6},{6,4},{8,10},{10,8},{12,14},{14,12},{1,3},{3,1},... | collective-permute-start | bytes 307208 | tf_op jit(solution)/shard_map/ppermute | solution.py:957
  7.1 3.6 %collective-permute-start.2 = (bf16[400,128]{1,0:T(8,128)(2,1)S(1)}, bf16[400,128]{1,0:T(8,128)(2,1)S(1)}, u32[]{:S(2)}, u32[]{:S(2)}) collective-permute-start(bf16[400,128]{1,0:T(8,128)(2,1)S(1)} %get-tuple-element.31), channel_id=1, source_target_pairs={{2,4},{4,2},{6,8},{8,6},{10,12},{12,10},{14,0},{0,14},{3,5},{5,3},... | collective-permute-start | bytes 307208 | tf_op jit(solution)/shard_map/ppermute | solution.py:958
  10.7 3.6 %third.1 = (f32[4,4,8,128,256]{4,3,2,1,0:T(8,128)S(1)}, bf16[1856,256]{1,0:T(8,128)(2,1)S(1)}, f32[12,128,128]{2,1,0:T(8,128)S(1)}, f32[128,128]{1,0:T(8,128)S(1)}) custom-call(f32[7,8,10,8,128]{4,3,2,1,0:T(8,128)S(1)} %get-tuple-element.23.ext_ref, f32[24,128]{1,0:T(8,128)S(1)} %get-tuple-element.24.table_ref, ...), custom_call_target="tpu_custom_call" | custom-call | flops 4000000000 | bytes 20000000 | tf_op jit(solution)/shard_map/third/pallas_call | solution.py:963
  14.3 0.0 collective-permute-done.1.ra_ref
  14.3 0.2 %collective-permute-done.2.rb_ref = bf16[400,128]{1,0:T(8,128)(2,1)S(1)} collective-permute-done((bf16[400,128]{1,0:T(8,128)(2,1)S(1)}, bf16[400,128]{1,0:T(8,128)(2,1)S(1)}, u32[]{:S(2)}, u32[]{:S(2)}) %collective-permute-start.2) | collective-permute-done | bytes 102432 | tf_op jit(solution)/shard_map/ppermute | solution.py:958
  14.5 6.6 %fourth.1 = f32[1,128]{1,0:T(1,128)} custom-call(f32[1]{0:T(128)S(6)} %copy.7.inv_ref, f32[4,4,8,128,256]{4,3,2,1,0:T(8,128)S(1)} %get-tuple-element.26.gs_ref, f32[12,128,128]{2,1,0:T(8,128)S(1)} %get-tuple-element.27.factor_ref, f32[128,128]{1,0:T(8,128)S(1)} %get-tuple-element.28.quad_ref, f32[7,8,10,8,128]{4,3,2,1,0:T(8,128)S(1)} %get-tuple-element.23.ext_ref, ...), custom_call_target="tpu_custom_call" | custom-call | tf_op jit(solution)/shard_map/fourth/pallas_call | solution.py:985
Async XLA Ops:
  2.1 1.6 %collective-permute-start = (bf16[592,128]{1,0:T(8,128)(2,1)S(1)}, bf16[592,128]{1,0:T(8,128)(2,1)S(1)}, u32[]{:S(2)}, u32[]{:S(2)}) collective-permute-start(bf16[592,128]{1,0:T(8,128)(2,1)S(1)} %get-tuple-element.22), channel_id=1, source_target_pairs={{0,1},{1,0},{2,3},{3,2},{4,5},{5,4},{6,7},{7,6},{8,9},{9,8},{10,11... | collective-permute-start | bytes 454664 | tf_op jit(solution)/shard_map/ppermute | solution.py:928
  4.3 10.0 %collective-permute-start.1 = (bf16[400,128]{1,0:T(8,128)(2,1)S(1)}, bf16[400,128]{1,0:T(8,128)(2,1)S(1)}, u32[]{:S(2)}, u32[]{:S(2)}) collective-permute-start(bf16[400,128]{1,0:T(8,128)(2,1)S(1)} %get-tuple-element.30), channel_id=1, source_target_pairs={{0,2},{2,0},{4,6},{6,4},{8,10},{10,8},{12,14},{14,12},{1,3},{3,1},... | collective-permute-start | bytes 307208 | tf_op jit(solution)/shard_map/ppermute | solution.py:957
  7.1 7.4 %collective-permute-start.2 = (bf16[400,128]{1,0:T(8,128)(2,1)S(1)}, bf16[400,128]{1,0:T(8,128)(2,1)S(1)}, u32[]{:S(2)}, u32[]{:S(2)}) collective-permute-start(bf16[400,128]{1,0:T(8,128)(2,1)S(1)} %get-tuple-element.31), channel_id=1, source_target_pairs={{2,4},{4,2},{6,8},{8,6},{10,12},{12,10},{14,0},{0,14},{3,5},{5,3},... | collective-permute-start | bytes 307208 | tf_op jit(solution)/shard_map/ppermute | solution.py:958
